TPU v7x, 512 devices: a whole 4x4x16 slice. The times are simulated.
512 devices in a mesh: grp: 16 (over z), row: 32 (over x, y, core).
Axes of the slice: x: 4, y: 4, z: 16, core: 2. Of those that a mesh axis runs over, the one named last changes fastest.
Arguments:
- design: bfloat16 [786432, 512], P(('grp', 'row')), may hold values from -0.29882812 to 0.29882812
- scales: bfloat16 [786432], P(('grp', 'row')), may hold values from 0.3984375 to 9.5
- buckets: int32 [786432], P(('grp', 'row')), may hold values from 0 to 1535
Outputs:
- sketch: float32 [24576, 512], P(('grp', 'row'))
- precond: float32 [512, 512], P('grp')
All inputs are finite; a program needn't handle non-finite values.
Results may differ from a plain program's by a relative error of at most 0.0003.
Values sent between devices are 32-bit elements; how exact they have to be, the bound alone decides.
No kernel may reach another device: no remote copies, remote signals or barrier semaphores. Data moves between devices by JAX's collectives and lax.ppermute only.
A program may use at most 64 MiB of HBM per device.

v0:
```python
import jax
import jax.numpy as jnp
from jax import lax
from jax.sharding import PartitionSpec as P


def partner_2(block, axis, stride):
    count = lax.axis_size(axis)
    route = []
    for low in range(count):
        high = low | 1 << stride
        if high != low and high < count:
            route += [(low, high), (high, low)]
    return lax.ppermute(block, axis, route)


def chol_upper(gram_matrix):
    return jnp.linalg.cholesky(gram_matrix).T


def self_gram(matrix):
    return lax.dot_general(
        matrix,
        matrix,
        (((0,), (0,)), ((), ())),
        precision=lax.Precision.HIGHEST,
        preferred_element_type=jnp.float32,
    )


def per_device(design, scales, buckets):
    row_count = design.shape[0]
    col_count = design.shape[1]
    row_parts = lax.axis_size("row")
    owned_rows = row_count // row_parts
    label_ids = lax.iota(jnp.int32, row_count)
    onehot_table = jnp.where(
        label_ids[:, None] == buckets[None, :], scales[None, :], jnp.zeros((), jnp.bfloat16)
    )
    partial_value = jnp.dot(onehot_table, design, preferred_element_type=jnp.float32).reshape(
        row_parts, owned_rows, col_count
    )
    arrived = lax.all_to_all(partial_value, "row", split_axis=0, concat_axis=0, tiled=True)
    sketch = jnp.sum(arrived, axis=0)
    local_gram = self_gram(sketch)
    group_gram = lax.psum(local_gram, "row")
    factor = chol_upper(group_gram)
    for bit_index in range(lax.axis_size("grp").bit_length() - 1):
        partner = partner_2(factor, "grp", bit_index)
        factor = chol_upper(self_gram(factor) + self_gram(partner))
    precond = factor / jnp.sqrt(jnp.float32(row_count * lax.axis_size("grp")))
    slab_rows = col_count // lax.axis_size("grp")
    slab_start = lax.axis_index("grp") * slab_rows
    precond_rows = lax.dynamic_slice_in_dim(precond, slab_start, slab_rows, 0)
    return (sketch, precond_rows)


def solution(mesh):
    in_specs = (P(("grp", "row"), None), P(("grp", "row")), P(("grp", "row")))
    out_specs = (P(("grp", "row"), None), P("grp", None))
    return jax.shard_map(
        per_device, mesh=mesh, in_specs=in_specs, out_specs=out_specs, check_vma=False
    )
```

profile of v0, /device:TPU:1, one launch (start us, length us, event | category | flops | bytes accessed | tf_op | source)
XLA Modules:
  0.0 933.6 jit_solution(3870824916542653050)
XLA Ops:
  11.9 49.7 %all_to_all.5 = f32[32,48,512]{2,1,0:T(8,128)} all-to-all(f32[32,48,512]{2,1,0:T(8,128)S(1)} %bitcast.130), channel_id=1, replica_groups=mesh['grp'=16,'row'=32] {'row'}, dimensions={0} | all-to-all | bytes 6291456 | tf_op jit(solution)/shard_map/all_to_all | solution.py:43
  65.8 134.5 %all-reduce.3.cloned.1.call-done = f32[512,512]{0,1:T(8,128)} async-done(((f32[512,512]{0,1:T(8,128)}), f32[512,512]{0,1:T(8,128)}) %all-reduce.3.cloned.1.call-update) | async-done | bytes 1048592 | tf_op jit(solution)/shard_map/psum | solution.py:46
  204.4 11.7 %cholesky.550 = f32[128,128]{1,0:T(8,128)S(1)} custom-call(f32[128,128]{1,0:T(8,128)S(1)} %cholesky.906), custom_call_target="Cholesky" | custom-call | tf_op jit(solution)/shard_map/jit(cholesky)/cholesky | solution.py:18
  216.2 9.8 %custom-call.32 = f32[1,128,128]{1,2,0:T(8,128)S(1)} custom-call(f32[1,128,128]{2,1,0:T(8,128)S(1)} %get-tuple-element.54), custom_call_target="InvertDiagBlocksLowerTriangular" | custom-call | tf_op jit(solution)/shard_map/jit(cholesky)/cholesky | solution.py:18
  228.6 12.1 %cholesky.569 = f32[128,128]{1,0:T(8,128)S(1)} custom-call(f32[128,128]{1,0:T(8,128)S(1)} %cholesky.910), custom_call_target="Cholesky" | custom-call | tf_op jit(solution)/shard_map/jit(cholesky)/cholesky | solution.py:18
  240.7 9.8 %custom-call.33 = f32[1,128,128]{1,2,0:T(8,128)S(1)} custom-call(f32[1,128,128]{2,1,0:T(8,128)S(1)} %get-tuple-element.51), custom_call_target="InvertDiagBlocksLowerTriangular" | custom-call | tf_op jit(solution)/shard_map/jit(cholesky)/cholesky | solution.py:18
  252.1 11.7 %cholesky.590 = f32[128,128]{1,0:T(8,128)S(1)} custom-call(f32[128,128]{1,0:T(8,128)S(1)} %cholesky.915), custom_call_target="Cholesky" | custom-call | tf_op jit(solution)/shard_map/jit(cholesky)/cholesky | solution.py:18
  275.8 11.9 %cholesky.607 = f32[128,128]{1,0:T(8,128)S(1)} custom-call(f32[128,128]{1,0:T(8,128)S(1)} %convolution_subtract_fusion.2), custom_call_target="Cholesky" | custom-call | tf_op jit(solution)/shard_map/jit(cholesky)/cholesky | solution.py:18
  296.9 20.7 %collective-permute-done = f32[512,512]{0,1:T(8,128)S(1)} collective-permute-done((f32[512,512]{0,1:T(8,128)S(1)}, f32[512,512]{0,1:T(8,128)S(1)}, u32[]{:S(2)}, u32[]{:S(2)}) %collective-permute-start) | collective-permute-done | bytes 1048608 | tf_op jit(solution)/shard_map/ppermute | solution.py:14
  323.2 11.7 %cholesky.622 = f32[128,128]{1,0:T(8,128)S(1)} custom-call(f32[128,128]{1,0:T(8,128)S(1)} %cholesky.919), custom_call_target="Cholesky" | custom-call | tf_op jit(solution)/shard_map/jit(cholesky)/cholesky | solution.py:18
  335.1 9.8 %custom-call.35 = f32[1,128,128]{1,2,0:T(8,128)S(1)} custom-call(f32[1,128,128]{2,1,0:T(8,128)S(1)} %get-tuple-element.44), custom_call_target="InvertDiagBlocksLowerTriangular" | custom-call | tf_op jit(solution)/shard_map/jit(cholesky)/cholesky | solution.py:18
  347.5 12.1 %cholesky.641 = f32[128,128]{1,0:T(8,128)S(1)} custom-call(f32[128,128]{1,0:T(8,128)S(1)} %cholesky.923), custom_call_target="Cholesky" | custom-call | tf_op jit(solution)/shard_map/jit(cholesky)/cholesky | solution.py:18
  372.3 11.7 %cholesky.662 = f32[128,128]{1,0:T(8,128)S(1)} custom-call(f32[128,128]{1,0:T(8,128)S(1)} %cholesky.928), custom_call_target="Cholesky" | custom-call | tf_op jit(solution)/shard_map/jit(cholesky)/cholesky | solution.py:18
  396.1 11.7 %cholesky.679 = f32[128,128]{1,0:T(8,128)S(1)} custom-call(f32[128,128]{1,0:T(8,128)S(1)} %slice_subtract_fusion.11), custom_call_target="Cholesky" | custom-call | tf_op jit(solution)/shard_map/jit(cholesky)/cholesky | solution.py:18
  417.4 43.2 %collective-permute-done.1 = f32[512,512]{0,1:T(8,128)S(1)} collective-permute-done((f32[512,512]{0,1:T(8,128)S(1)}, f32[512,512]{0,1:T(8,128)S(1)}, u32[]{:S(2)}, u32[]{:S(2)}) %collective-permute-start.1) | collective-permute-done | bytes 1048608 | tf_op jit(solution)/shard_map/ppermute | solution.py:14
  466.3 11.7 %cholesky.694 = f32[128,128]{1,0:T(8,128)S(1)} custom-call(f32[128,128]{1,0:T(8,128)S(1)} %cholesky.932), custom_call_target="Cholesky" | custom-call | tf_op jit(solution)/shard_map/jit(cholesky)/cholesky | solution.py:18
  478.1 9.8 %custom-call.38 = f32[1,128,128]{1,2,0:T(8,128)S(1)} custom-call(f32[1,128,128]{2,1,0:T(8,128)S(1)} %get-tuple-element.34), custom_call_target="InvertDiagBlocksLowerTriangular" | custom-call | tf_op jit(solution)/shard_map/jit(cholesky)/cholesky | solution.py:18
  490.5 12.1 %cholesky.713 = f32[128,128]{1,0:T(8,128)S(1)} custom-call(f32[128,128]{1,0:T(8,128)S(1)} %cholesky.936), custom_call_target="Cholesky" | custom-call | tf_op jit(solution)/shard_map/jit(cholesky)/cholesky | solution.py:18
  515.4 11.7 %cholesky.734 = f32[128,128]{1,0:T(8,128)S(1)} custom-call(f32[128,128]{1,0:T(8,128)S(1)} %cholesky.941), custom_call_target="Cholesky" | custom-call | tf_op jit(solution)/shard_map/jit(cholesky)/cholesky | solution.py:18
  539.2 11.7 %cholesky.751 = f32[128,128]{1,0:T(8,128)S(1)} custom-call(f32[128,128]{1,0:T(8,128)S(1)} %slice_subtract_fusion.10), custom_call_target="Cholesky" | custom-call | tf_op jit(solution)/shard_map/jit(cholesky)/cholesky | solution.py:18
  563.6 88.1 %collective-permute-done.2 = f32[512,512]{0,1:T(8,128)S(1)} collective-permute-done((f32[512,512]{0,1:T(8,128)S(1)}, f32[512,512]{0,1:T(8,128)S(1)}, u32[]{:S(2)}, u32[]{:S(2)}) %collective-permute-start.2) | collective-permute-done | bytes 1048608 | tf_op jit(solution)/shard_map/ppermute | solution.py:14
  657.4 11.7 %cholesky.766 = f32[128,128]{1,0:T(8,128)S(1)} custom-call(f32[128,128]{1,0:T(8,128)S(1)} %cholesky.945), custom_call_target="Cholesky" | custom-call | tf_op jit(solution)/shard_map/jit(cholesky)/cholesky | solution.py:18
  669.3 9.8 %custom-call.41 = f32[1,128,128]{1,2,0:T(8,128)S(1)} custom-call(f32[1,128,128]{2,1,0:T(8,128)S(1)} %get-tuple-element.24), custom_call_target="InvertDiagBlocksLowerTriangular" | custom-call | tf_op jit(solution)/shard_map/jit(cholesky)/cholesky | solution.py:18
  681.6 12.1 %cholesky.785 = f32[128,128]{1,0:T(8,128)S(1)} custom-call(f32[128,128]{1,0:T(8,128)S(1)} %cholesky.949), custom_call_target="Cholesky" | custom-call | tf_op jit(solution)/shard_map/jit(cholesky)/cholesky | solution.py:18
  706.5 11.7 %cholesky.806 = f32[128,128]{1,0:T(8,128)S(1)} custom-call(f32[128,128]{1,0:T(8,128)S(1)} %cholesky.954), custom_call_target="Cholesky" | custom-call | tf_op jit(solution)/shard_map/jit(cholesky)/cholesky | solution.py:18
  730.3 11.7 %cholesky.823 = f32[128,128]{1,0:T(8,128)S(1)} custom-call(f32[128,128]{1,0:T(8,128)S(1)} %slice_subtract_fusion.9), custom_call_target="Cholesky" | custom-call | tf_op jit(solution)/shard_map/jit(cholesky)/cholesky | solution.py:18
  746.5 11.1 %collective-permute-start.3 = (f32[512,512]{0,1:T(8,128)}, f32[512,512]{0,1:T(8,128)}, u32[]{:S(2)}, u32[]{:S(2)}) collective-permute-start(f32[512,512]{0,1:T(8,128)} %fusion.15), channel_id=1, source_target_pairs={{0,256},{256,0},{32,288},{288,32},{64,320},{320,64},{96,352},{352,... | collective-permute-start | bytes 3145736 | tf_op jit(solution)/shard_map/ppermute | solution.py:14
  759.6 70.5 %collective-permute-done.3 = f32[512,512]{0,1:T(8,128)} collective-permute-done((f32[512,512]{0,1:T(8,128)}, f32[512,512]{0,1:T(8,128)}, u32[]{:S(2)}, u32[]{:S(2)}) %collective-permute-start.3) | collective-permute-done | bytes 1048608 | tf_op jit(solution)/shard_map/ppermute | solution.py:14
  837.3 11.7 %cholesky.838 = f32[128,128]{1,0:T(8,128)S(1)} custom-call(f32[128,128]{1,0:T(8,128)S(1)} %cholesky.958), custom_call_target="Cholesky" | custom-call | tf_op jit(solution)/shard_map/jit(cholesky)/cholesky | solution.py:18
  861.9 11.9 %cholesky.857 = f32[128,128]{1,0:T(8,128)S(1)} custom-call(f32[128,128]{1,0:T(8,128)S(1)} %cholesky.962), custom_call_target="Cholesky" | custom-call | tf_op jit(solution)/shard_map/jit(cholesky)/cholesky | solution.py:18
  886.6 11.7 %cholesky.878 = f32[128,128]{1,0:T(8,128)S(1)} custom-call(f32[128,128]{1,0:T(8,128)S(1)} %cholesky.967), custom_call_target="Cholesky" | custom-call | tf_op jit(solution)/shard_map/jit(cholesky)/cholesky | solution.py:18
  910.5 11.7 %cholesky.895 = f32[128,128]{1,0:T(8,128)S(1)} custom-call(f32[128,128]{1,0:T(8,128)S(1)} %slice_subtract_fusion.8), custom_call_target="Cholesky" | custom-call | tf_op jit(solution)/shard_map/jit(cholesky)/cholesky | solution.py:18
  (148 shorter events, 202.8 us)
Async XLA Ops:
  7.2 1.4 copy-start
  7.2 193.2 %all-reduce.3.cloned.1.call-start = ((), (), s32[]{:S(2)}) async-start(), calls=%async_computation.1 | async-start | bytes 2097152 | tf_op jit(solution)/shard_map/psum | solution.py:46
  63.7 139.6 %copy-start.6 = (f32[48,512]{1,0:T(8,128)}, f32[48,512]{1,0:T(8,128)S(1)}, u32[]{:S(2)}) copy-start(f32[48,512]{1,0:T(8,128)S(1)} %reduce_sum.9) | copy-start | bytes 294916
  203.4 1.0 copy-start.5
  291.8 25.8 %collective-permute-start = (f32[512,512]{0,1:T(8,128)S(1)}, f32[512,512]{0,1:T(8,128)S(1)}, u32[]{:S(2)}, u32[]{:S(2)}) collective-permute-start(f32[512,512]{0,1:T(8,128)S(1)} %fusion.24), channel_id=1, source_target_pairs={{0,32},{32,0},{64,96},{96,64},{128,160},{160,128},{192,224},{224,1... | collective-permute-start | bytes 3145736 | tf_op jit(solution)/shard_map/ppermute | solution.py:14
  322.2 1.0 copy-start.2
  411.3 49.3 %collective-permute-start.1 = (f32[512,512]{0,1:T(8,128)S(1)}, f32[512,512]{0,1:T(8,128)S(1)}, u32[]{:S(2)}, u32[]{:S(2)}) collective-permute-start(f32[512,512]{0,1:T(8,128)S(1)} %fusion.21), channel_id=1, source_target_pairs={{0,64},{64,0},{32,96},{96,32},{128,192},{192,128},{160,224},{224,1... | collective-permute-start | bytes 3145736 | tf_op jit(solution)/shard_map/ppermute | solution.py:14
  465.3 1.0 copy-start.3
  554.4 97.4 %collective-permute-start.2 = (f32[512,512]{0,1:T(8,128)S(1)}, f32[512,512]{0,1:T(8,128)S(1)}, u32[]{:S(2)}, u32[]{:S(2)}) collective-permute-start(f32[512,512]{0,1:T(8,128)S(1)} %fusion.18), channel_id=1, source_target_pairs={{0,128},{128,0},{32,160},{160,32},{64,192},{192,64},{96,224},{224,... | collective-permute-start | bytes 3145736 | tf_op jit(solution)/shard_map/ppermute | solution.py:14
  656.4 1.0 copy-start.4
  746.5 83.6 %collective-permute-start.3 = (f32[512,512]{0,1:T(8,128)}, f32[512,512]{0,1:T(8,128)}, u32[]{:S(2)}, u32[]{:S(2)}) collective-permute-start(f32[512,512]{0,1:T(8,128)} %fusion.15), channel_id=1, source_target_pairs={{0,256},{256,0},{32,288},{288,32},{64,320},{320,64},{96,352},{352,... | collective-permute-start | bytes 3145736 | tf_op jit(solution)/shard_map/ppermute | solution.py:14
  836.3 1.0 copy-start.1
Sparse Core Ops, SparseCore 0:
  65.9 134.3 all-reduce.2
where the time goes:
time: 938 us; the launch traced here: 934 us
  other arithmetic  408 us (43%)
  waiting for transfers between devices  357 us (38%)
  matrix products  50.3 us (5%)
  blocking collectives  49.7 us (5%)
  between operations  28 us (3%)
  starting transfers between devices  25.9 us (3%)
  local copies, waits for them, and re-layouts  14.7 us (2%)
    another operation x74, other arithmetic, chol_upper(): return jnp.linalg.cholesky(gram_matrix).T  397 us
    ppermute x4, waiting for transfers between devices, partner_2(): return lax.ppermute(block, axis, route)  222 us
    psum x1, waiting for transfers between devices, per_device(): group_gram = lax.psum(local_gram, 'row')  135 us
    all_to_all x1, blocking collectives, per_device(): lax.all_to_all(partial_value, 'row', split_axis=0, concat_axis=0, tiled=T...  49.7 us
    another operation x30, matrix products, chol_upper(): return jnp.linalg.cholesky(gram_matrix).T  28.3 us
    ppermute x4, starting transfers between devices, partner_2(): return lax.ppermute(block, axis, route)  25.8 us
  transfers between devices with their start and end apart: 5, of which 5 were waited for; matrix products, arithmetic and copies ran while one was open for 1% of the time, Pallas kernels for 0%

commit v1 on v0

v1 whole, which is shorter than its diff:
```python
import jax
import jax.numpy as jnp
from jax import lax
from jax.sharding import Mesh
from jax.sharding import PartitionSpec as P

TILE = 128
ALL = ("zh", "zl", "x", "y", "core")


def blocks_of(size):
    count = size // TILE
    return [(i, j) for i in range(count) for j in range(i, count)]


def exchange(value, axes):
    return lax.all_to_all(value, axes, split_axis=0, concat_axis=0, tiled=True)


def spread(value, axes):
    count = lax.axis_size(axes)
    return exchange(jnp.broadcast_to(value[None], (count,) + value.shape), axes)


def self_gram(matrix):
    return lax.dot_general(
        matrix,
        matrix,
        (((0,), (0,)), ((), ())),
        precision=lax.Precision.HIGHEST,
        preferred_element_type=jnp.float32,
    )


def bucket_sums(design, scales, buckets, core, chips, owned):
    slots = lax.broadcasted_iota(jnp.int32, (chips, owned), 0) * (2 * owned) + core * owned
    slots = (slots + lax.broadcasted_iota(jnp.int32, (chips, owned), 1)).reshape(-1)
    table = jnp.where(slots[:, None] == buckets[None, :], scales[None, :], jnp.zeros((), jnp.bfloat16))
    return jnp.dot(table, design, preferred_element_type=jnp.float32)


def per_device(design, scales, buckets):
    rows, cols = design.shape
    chips = lax.axis_size(("x", "y"))
    owned = rows // (2 * chips)
    core = lax.axis_index("core")
    theirs = bucket_sums(design, scales, buckets, 1 - core, chips, owned)
    from_pair = lax.ppermute(theirs, "core", [(0, 1), (1, 0)])
    ours = bucket_sums(design, scales, buckets, core, chips, owned)
    paired = (ours + from_pair).reshape(chips, owned, cols)
    sketch = jnp.sum(exchange(paired, ("x", "y")), axis=0)
    local = self_gram(sketch)
    pairs = blocks_of(cols)
    packed = jnp.stack(
        [local[i * TILE : (i + 1) * TILE, j * TILE : (j + 1) * TILE] for i, j in pairs]
    )
    devices = 2 * chips
    packed = packed.reshape(devices, -1, TILE)
    piece = jnp.sum(exchange(packed, ("x", "y", "core")), axis=0)
    piece = jnp.sum(spread(piece, ("zl",)), axis=0)
    piece = jnp.sum(spread(piece, ("zh",)), axis=0)
    whole = spread(piece, ("x", "y", "core")).reshape(len(pairs), TILE, TILE)
    at = {pair: n for n, pair in enumerate(pairs)}
    count = cols // TILE
    gram = jnp.concatenate(
        [
            jnp.concatenate(
                [whole[at[i, j]] if i <= j else whole[at[j, i]].T for j in range(count)], axis=1
            )
            for i in range(count)
        ],
        axis=0,
    )
    groups = lax.axis_size(("zh", "zl"))
    precond = jnp.linalg.cholesky(gram, symmetrize_input=False).T / jnp.sqrt(jnp.float32(rows * groups))
    slab = cols // groups
    start = lax.axis_index(("zh", "zl")) * slab
    return sketch, lax.dynamic_slice_in_dim(precond, start, slab, 0)


def solution(mesh):
    fine = Mesh(mesh.devices.reshape(4, 4, 4, 4, 2), ALL)
    rows = ALL
    in_specs = (P(rows, None), P(rows), P(rows))
    out_specs = (P(rows, None), P(("zh", "zl"), None))
    return jax.shard_map(
        per_device, mesh=fine, in_specs=in_specs, out_specs=out_specs, check_vma=False
    )
```

time: 938 us -> 211 us (0.22)
  waiting for transfers between devices: 357 us -> 15.7 us
  other arithmetic: 408 us -> 83.5 us
  matrix products: 50.3 us -> 9.9 us
  blocking collectives: 49.7 us -> 75.4 us
  between operations: 28 us -> 3.63 us
  starting transfers between devices: 25.9 us -> 15.2 us
    another operation x74 -> x14, other arithmetic: 397 us -> 83 us  [per_device(): jnp.linalg.cholesky(gram, symmetrize_input=False)]
    ppermute x4 -> x1, waiting for transfers between devices: 222 us -> 2.98 us  [per_device(): from_pair = lax.ppermute(theirs, 'core', [(0, 1), (1, 0)])]
    psum x1 -> x0, waiting for transfers between devices: 135 us -> none  [per_device(): group_gram = lax.psum(local_gram, 'row')]
    all_to_all x1 -> x4, blocking collectives: 49.7 us -> 75.4 us  [exchange(): return lax.all_to_all(value, axes, split_axis=0, concat_axis=0, tiled=True)]
    another operation x30 -> x6, matrix products: 28.3 us -> 3.84 us  [per_device(): jnp.linalg.cholesky(gram, symmetrize_input=False)]
    dot_general x9 -> x1, matrix products: 18.7 us -> 1.03 us  [self_gram(): lax.dot_general(matrix, matrix, (((0,), (0,)), ((), ())), precision=lax.P...]
    ppermute x4 -> x1, starting transfers between devices: 25.8 us -> 8.81 us  [per_device(): from_pair = lax.ppermute(theirs, 'core', [(0, 1), (1, 0)])]
    all_to_all x0 -> x1, waiting for transfers between devices: none -> 12.8 us  [exchange(): return lax.all_to_all(value, axes, split_axis=0, concat_axis=0, tiled=True)]
  transfers between devices with their start and end apart: 5 -> 2, of which waited for: 5 -> 2; matrix products, arithmetic and copies ran while one was open for 1% -> 0% of each run, Pallas kernels for 0% -> 0%
where the time goes in v1:
time: 211 us; the launch traced here: 210 us
  other arithmetic  83.5 us (40%)
  blocking collectives  75.4 us (36%)
  waiting for transfers between devices  15.7 us (7%)
  starting transfers between devices  15.2 us (7%)
  matrix products  9.9 us (5%)
  local copies, waits for them, and re-layouts  7.13 us (3%)
  between operations  3.63 us (2%)
    another operation x14, other arithmetic, per_device(): jnp.linalg.cholesky(gram, symmetrize_input=False)  83 us
    all_to_all x4, blocking collectives, exchange(): return lax.all_to_all(value, axes, split_axis=0, concat_axis=0, tiled=True)  75.4 us
    all_to_all x1, waiting for transfers between devices, exchange(): return lax.all_to_all(value, axes, split_axis=0, concat_axis=0, tiled=True)  12.8 us
    ppermute x1, starting transfers between devices, per_device(): from_pair = lax.ppermute(theirs, 'core', [(0, 1), (1, 0)])  8.81 us
    all_to_all x1, starting transfers between devices, exchange(): return lax.all_to_all(value, axes, split_axis=0, concat_axis=0, tiled=True)  6.38 us
    dot_general x2, matrix products, bucket_sums(): return jnp.dot(table, design, preferred_element_type=jnp.float32)  5.03 us
  transfers between devices with their start and end apart: 2, of which 2 were waited for; matrix products, arithmetic and copies ran while one was open for 0% of the time, Pallas kernels for 0%

profile of v1, /device:TPU:1, one launch (start us, length us, event | category | flops | bytes accessed | tf_op | source)
XLA Modules:
  0.0 210.5 jit_solution(14163982914123808441)
XLA Ops:
  0.8 1.2 copy-done
  2.0 2.2 %fusion.1 = f32[768,512]{1,0:T(8,128)S(1)} fusion(bf16[1536,512]{1,0:T(8,128)(2,1)S(1)} %copy-done, s32[1536]{0:T(1024)} %param.5, s32[768]{0:T(1024)S(1)} %add.84, bf16[1536]{0:T(1024)(128)(2,1)} %param.4), kind=kOutput, calls=%fused_computation.3 | convolution fusion | flops 1210318848 | bytes 3158016 | tf_op jit(solution)/shard_map/dot_general | solution.py:39
  4.2 8.8 %collective-permute-start = (f32[768,512]{1,0:T(8,128)S(1)}, f32[768,512]{1,0:T(8,128)}, u32[]{:S(2)}, u32[]{:S(2)}) collective-permute-start(f32[768,512]{1,0:T(8,128)S(1)} %fusion.1), channel_id=1, source_target_pairs={{0,1},{1,0},{2,3},{3,2},{4,5},{5,4},{6,7},{7,6},{8,9},{9,8},{10,11... | collective-permute-start | bytes 4718600 | tf_op jit(solution)/shard_map/ppermute | solution.py:48
  13.2 3.0 %collective-permute-done = f32[768,512]{1,0:T(8,128)} collective-permute-done((f32[768,512]{1,0:T(8,128)S(1)}, f32[768,512]{1,0:T(8,128)}, u32[]{:S(2)}, u32[]{:S(2)}) %collective-permute-start) | collective-permute-done | bytes 1572896 | tf_op jit(solution)/shard_map/ppermute | solution.py:48
  16.2 2.8 %fusion.6 = f32[768,512]{1,0:T(8,128)S(1)} fusion(f32[768,512]{1,0:T(8,128)} %collective-permute-done, bf16[1536,512]{1,0:T(8,128)(2,1)S(1)} %copy-done, s32[1536]{0:T(1024)S(1)} %copy-done.10, s32[768]{0:T(1024)S(1)} %add.80, bf16[1536]{0:T(1024)(128)(2,1)S(1)} %copy-done.11), kind=kOutput, calls=%fused_computation.8 | convolution fusion | flops 1210712064 | bytes 4730880 | tf_op jit(solution)/shard_map/dot_general | solution.py:39
  19.1 24.1 %all_to_all.25 = f32[16,48,512]{2,1,0:T(8,128)S(1)} all-to-all(f32[16,48,512]{2,1,0:T(8,128)S(1)} %bitcast.104), channel_id=1, replica_groups=mesh['zh'=4,'zl'=4,'x'=4,'y'=4,'core'=2] {'x','y'}, dimensions={0} | all-to-all | bytes 3145728 | tf_op jit(solution)/shard_map/all_to_all | solution.py:17
  43.3 1.0 fusion.47
  44.5 18.4 %all_to_all.26 = f32[32,40,128]{2,1,0:T(8,128)S(1)} all-to-all(f32[32,40,128]{2,1,0:T(8,128)S(1)} %bitcast.105), channel_id=1, replica_groups=mesh['zh'=4,'zl'=4,'x'=4,'y'=4,'core'=2] {'x','y','core'}, dimensions={0} | all-to-all | bytes 1310720 | tf_op jit(solution)/shard_map/all_to_all | solution.py:17
  63.0 8.7 %all_to_all.27 = f32[4,40,128]{2,1,0:T(8,128)S(1)} all-to-all(f32[4,40,128]{2,1,0:T(8,128)S(1)} %broadcast_in_dim.42), channel_id=1, replica_groups=mesh['zh'=4,'zl'=4,'x'=4,'y'=4,'core'=2] {'zl'}, dimensions={0} | all-to-all | bytes 163840 | tf_op jit(solution)/shard_map/all_to_all | solution.py:17
  71.7 24.2 %all_to_all.28 = f32[4,40,128]{2,1,0:T(8,128)S(1)} all-to-all(f32[4,40,128]{2,1,0:T(8,128)S(1)} %broadcast_in_dim.43), channel_id=1, replica_groups=mesh['zh'=4,'zl'=4,'x'=4,'y'=4,'core'=2] {'zh'}, dimensions={0} | all-to-all | bytes 163840 | tf_op jit(solution)/shard_map/all_to_all | solution.py:17
  95.9 0.9 broadcast_in_dim.44
  96.8 6.4 %all-to-all-start.4 = ((f32[32,40,128]{2,1,0:T(8,128)}), f32[32,40,128]{2,1,0:T(8,128)S(1)}, u32[]{:S(2)}, u32[]{:S(2)}) async-start(f32[32,40,128]{2,1,0:T(8,128)} %broadcast_in_dim.44), calls=%async_computation.4 | async-start | bytes 1310720 | tf_op jit(solution)/shard_map/all_to_all | solution.py:17
  103.2 12.8 %all-to-all-done.4 = f32[32,40,128]{2,1,0:T(8,128)S(1)} async-done(((f32[32,40,128]{2,1,0:T(8,128)}), f32[32,40,128]{2,1,0:T(8,128)S(1)}, u32[]{:S(2)}, u32[]{:S(2)}) %all-to-all-start.4) | async-done | bytes 655392 | tf_op jit(solution)/shard_map/all_to_all | solution.py:17
  116.7 11.7 %cholesky.101 = f32[128,128]{1,0:T(8,128)S(1)} custom-call(f32[128,128]{1,0:T(8,128)S(1)} %get-tuple-element.18), custom_call_target="Cholesky" | custom-call | tf_op jit(solution)/shard_map/jit(cholesky)/cholesky | solution.py:75
  128.4 9.8 %custom-call.27 = f32[1,128,128]{1,2,0:T(8,128)S(1)} custom-call(f32[1,128,128]{2,1,0:T(8,128)S(1)} %get-tuple-element.28), custom_call_target="InvertDiagBlocksLowerTriangular" | custom-call | tf_op jit(solution)/shard_map/jit(cholesky)/cholesky | solution.py:75
  138.7 0.5 convolution_subtract_fusion
  139.3 0.8 copy.21
  140.1 1.0 cholesky.219
  141.0 0.6 cholesky.261
  141.7 13.2 %cholesky.212 = f32[128,128]{1,0:T(8,128)} custom-call(f32[128,128]{1,0:T(8,128)} %cholesky.261), custom_call_target="Cholesky" | custom-call | tf_op jit(solution)/shard_map/jit(cholesky)/cholesky | solution.py:75
  154.8 0.9 constant_dynamic-update-slice_fusion.2
  155.8 1.5 select_reduce_fusion.2
  157.3 11.5 %custom-call.28 = f32[1,128,128]{1,2,0:T(8,128)} custom-call(f32[1,128,128]{2,1,0:T(8,128)} %get-tuple-element.25), custom_call_target="InvertDiagBlocksLowerTriangular" | custom-call | tf_op jit(solution)/shard_map/jit(cholesky)/cholesky | solution.py:75
  168.7 1.1 convolution_dynamic-update-slice_fusion
  169.8 1.3 convolution_subtract_fusion.1
  171.1 11.7 %cholesky.233 = f32[128,128]{1,0:T(8,128)S(1)} custom-call(f32[128,128]{1,0:T(8,128)S(1)} %cholesky.265), custom_call_target="Cholesky" | custom-call | tf_op jit(solution)/shard_map/jit(cholesky)/cholesky | solution.py:75
  182.9 0.7 compare_reduce_fusion.1
  183.6 9.8 %custom-call.29 = f32[1,128,128]{1,2,0:T(8,128)S(1)} custom-call(f32[1,128,128]{2,1,0:T(8,128)S(1)} %get-tuple-element.22), custom_call_target="InvertDiagBlocksLowerTriangular" | custom-call | tf_op jit(solution)/shard_map/jit(cholesky)/cholesky | solution.py:75
  194.0 11.7 %cholesky.249 = f32[128,128]{1,0:T(8,128)S(1)} custom-call(f32[128,128]{1,0:T(8,128)S(1)} %convolution_subtract_fusion.2), custom_call_target="Cholesky" | custom-call | tf_op jit(solution)/shard_map/jit(cholesky)/cholesky | solution.py:75
  205.7 0.6 compare_reduce_fusion
  206.4 0.7 compare_reduce_fusion.2
  209.7 0.7 copy.24
  (60 shorter events, 2.5 us)
Async XLA Ops:
  0.6 1.4 copy-start
  2.0 14.2 %copy-start.10 = (s32[1536]{0:T(1024)S(1)}, s32[1536]{0:T(1024)}, u32[]{:S(2)}) copy-start(s32[1536]{0:T(1024)} %param.5) | copy-start | bytes 18436
  2.0 14.2 %copy-start.11 = (bf16[1536]{0:T(1024)(128)(2,1)S(1)}, bf16[1536]{0:T(1024)(128)(2,1)}, u32[]{:S(2)}) copy-start(bf16[1536]{0:T(1024)(128)(2,1)} %param.4) | copy-start | bytes 9220
  4.2 12.0 %collective-permute-start = (f32[768,512]{1,0:T(8,128)S(1)}, f32[768,512]{1,0:T(8,128)}, u32[]{:S(2)}, u32[]{:S(2)}) collective-permute-start(f32[768,512]{1,0:T(8,128)S(1)} %fusion.1), channel_id=1, source_target_pairs={{0,1},{1,0},{2,3},{3,2},{4,5},{5,4},{6,7},{7,6},{8,9},{9,8},{10,11... | collective-permute-start | bytes 4718600 | tf_op jit(solution)/shard_map/ppermute | solution.py:48
  43.3 19.7 %copy-start.1 = (f32[48,512]{1,0:T(8,128)}, f32[48,512]{1,0:T(8,128)S(1)}, u32[]{:S(2)}) copy-start(f32[48,512]{1,0:T(8,128)S(1)} %reduce_sum.36) | copy-start | bytes 294916
  96.8 19.1 %all-to-all-start.4 = ((f32[32,40,128]{2,1,0:T(8,128)}), f32[32,40,128]{2,1,0:T(8,128)S(1)}, u32[]{:S(2)}, u32[]{:S(2)}) async-start(f32[32,40,128]{2,1,0:T(8,128)} %broadcast_in_dim.44), calls=%async_computation.4 | async-start | bytes 1310720 | tf_op jit(solution)/shard_map/all_to_all | solution.py:17
  116.0 23.1 %copy-start.2 = (f32[128,128]{1,0:T(8,128)}, f32[128,128]{1,0:T(8,128)S(1)}, u32[]{:S(2)}) copy-start(f32[128,128]{1,0:T(8,128)S(1)} %get-tuple-element.12) | copy-start | bytes 196612
  116.0 23.1 %copy-start.3 = (f32[128,128]{1,0:T(8,128)}, f32[128,128]{1,0:T(8,128)S(1)}, u32[]{:S(2)}) copy-start(f32[128,128]{1,0:T(8,128)S(1)} %get-tuple-element.13) | copy-start | bytes 196612
  116.3 23.0 %copy-start.4 = (f32[128,128]{1,0:T(8,128)}, f32[128,128]{1,0:T(8,128)S(1)}, u32[]{:S(2)}) copy-start(f32[128,128]{1,0:T(8,128)S(1)} %copy.17) | copy-start | bytes 196612
  116.4 22.9 %copy-start.5 = (f32[128,128]{1,0:T(8,128)}, f32[128,128]{1,0:T(8,128)S(1)}, u32[]{:S(2)}) copy-start(f32[128,128]{1,0:T(8,128)S(1)} %copy.19) | copy-start | bytes 196612
  116.5 22.8 %copy-start.6 = (f32[128,128]{1,0:T(8,128)}, f32[128,128]{1,0:T(8,128)S(1)}, u32[]{:S(2)}) copy-start(f32[128,128]{1,0:T(8,128)S(1)} %copy.20) | copy-start | bytes 196612
  116.6 22.7 %copy-start.7 = (f32[128,128]{1,0:T(8,128)}, f32[128,128]{1,0:T(8,128)S(1)}, u32[]{:S(2)}) copy-start(f32[128,128]{1,0:T(8,128)S(1)} %copy.18) | copy-start | bytes 196612
  116.7 22.6 %copy-start.8 = (f32[128,128]{1,0:T(8,128)}, f32[128,128]{1,0:T(8,128)S(1)}, u32[]{:S(2)}) copy-start(f32[128,128]{1,0:T(8,128)S(1)} %copy.16) | copy-start | bytes 196612
  128.4 9.9 %copy-start.9 = (f32[128,128]{1,0:T(8,128)}, f32[128,128]{1,0:T(8,128)S(1)}, u32[]{:S(2)}) copy-start(f32[128,128]{1,0:T(8,128)S(1)} %cholesky.101) | copy-start | bytes 196612

commit v2 on v1

--- a/solution.py
+++ b/solution.py
@@ -1,10 +1,16 @@
+import functools
+import math
+
 import jax
 import jax.numpy as jnp
 from jax import lax
+from jax.experimental import pallas as pl
+from jax.experimental.pallas import tpu as pltpu
 from jax.sharding import Mesh
 from jax.sharding import PartitionSpec as P
 
 TILE = 128
+SUB = 8
 ALL = ("zh", "zl", "x", "y", "core")
 
 
@@ -39,6 +45,111 @@
     return jnp.dot(table, design, preferred_element_type=jnp.float32)
 
 
+def terms(value):
+    high = value.astype(jnp.bfloat16).astype(jnp.float32)
+    rest = value - high
+    middle = rest.astype(jnp.bfloat16).astype(jnp.float32)
+    return high, middle, rest - middle
+
+
+def rank_update(left, right):
+    a, b, c = terms(left)
+    d, e, f = terms(right)
+    tall = jnp.concatenate([a, a, b, b, a, c], 0).astype(jnp.bfloat16)
+    wide = jnp.concatenate([d, e, d, e, f, d], 0).astype(jnp.bfloat16)
+    return lax.dot_general(tall, wide, (((0,), (0,)), ((), ())), preferred_element_type=jnp.float32)
+
+
+def fill(value):
+    return jnp.broadcast_to(value, (SUB, TILE))
+
+
+def factor_kernel(slab_ref, gram_ref, out_ref, work, *, count, scale):
+    at = {pair: n for n, pair in enumerate(blocks_of(count * TILE))}
+    work[...] = gram_ref[...]
+    for b in range(count):
+        js = range(b, count)
+        ahead = None
+        for top in range(0, TILE, SUB):
+            rows = ahead
+            if rows is None:
+                rows = [{j: fill(work[at[b, j], top + t : top + t + 1, :]) for j in js} for t in range(SUB)]
+            pivot = {
+                (t, u): fill(rows[t][b][:, top + u : top + u + 1]) for t in range(SUB) for u in range(t, SUB)
+            }
+            done = []
+            for t in range(SUB):
+                inverse = lax.rsqrt(pivot[t, t])
+                coef = {u: pivot[t, u] * inverse for u in range(t + 1, SUB)}
+                for u in range(t + 1, SUB):
+                    for v in range(u, SUB):
+                        pivot[u, v] = pivot[u, v] - coef[u] * coef[v]
+                done.append({j: rows[t][j] * inverse for j in js})
+                for u in range(t + 1, SUB):
+                    for j in js:
+                        rows[u][j] = rows[u][j] - coef[u] * done[t][j]
+            for t in range(SUB):
+                for j in js:
+                    work[at[b, j], top + t : top + t + 1, :] = done[t][j][0:1, :]
+            ahead = None
+            below = top + SUB
+            if below < TILE:
+                ahead = [
+                    {j: fill(work[at[b, j], below + u : below + u + 1, :]) for j in js} for u in range(SUB)
+                ]
+                for t in range(SUB):
+                    for u in range(SUB):
+                        coef = fill(done[t][b][:, below + u : below + u + 1])
+                        for j in js:
+                            ahead[u][j] = ahead[u][j] - coef * done[t][j]
+            later = top + 2 * SUB
+            if later < TILE:
+                left = work[at[b, b], top : top + SUB, :]
+                for j in js:
+                    update = rank_update(left, work[at[b, j], top : top + SUB, :])
+                    work[at[b, j], later:, :] = work[at[b, j], later:, :] - update[later:, :]
+        for i in range(b + 1, count):
+            for j in range(i, count):
+                work[at[i, j]] = work[at[i, j]] - lax.dot_general(
+                    work[at[b, i]],
+                    work[at[b, j]],
+                    (((0,), (0,)), ((), ())),
+                    precision=lax.Precision.HIGHEST,
+                    preferred_element_type=jnp.float32,
+                )
+    slab = slab_ref[0]
+    height = out_ref.shape[0]
+    per_tile = TILE // height
+    for i in range(count):
+
+        @pl.when(slab // per_tile == i)
+        def _():
+            start = pl.multiple_of((slab % per_tile) * height, height)
+            shape = (height, TILE)
+            for j in range(count):
+                if j < i:
+                    value = jnp.zeros(shape, jnp.float32)
+                else:
+                    value = work[at[i, j], pl.ds(start, height), :] * scale
+                if j == i:
+                    upper = lax.broadcasted_iota(jnp.int32, shape, 1) >= start + lax.broadcasted_iota(
+                        jnp.int32, shape, 0
+                    )
+                    value = jnp.where(upper, value, 0.0)
+                out_ref[:, j * TILE : (j + 1) * TILE] = value
+
+
+def factor_rows(slab, packed, height, cols, scale):
+    return pl.pallas_call(
+        functools.partial(factor_kernel, count=cols // TILE, scale=scale),
+        out_shape=jax.ShapeDtypeStruct((height, cols), jnp.float32),
+        in_specs=[pl.BlockSpec(memory_space=pltpu.SMEM), pl.BlockSpec(memory_space=pltpu.VMEM)],
+        out_specs=pl.BlockSpec(memory_space=pltpu.VMEM),
+        scratch_shapes=[pltpu.VMEM(packed.shape, jnp.float32)],
+        name="factor_rows",
+    )(slab.reshape(1), packed)
+
+
 def per_device(design, scales, buckets):
     rows, cols = design.shape
     chips = lax.axis_size(("x", "y"))
@@ -60,22 +171,10 @@
     piece = jnp.sum(spread(piece, ("zl",)), axis=0)
     piece = jnp.sum(spread(piece, ("zh",)), axis=0)
     whole = spread(piece, ("x", "y", "core")).reshape(len(pairs), TILE, TILE)
-    at = {pair: n for n, pair in enumerate(pairs)}
-    count = cols // TILE
-    gram = jnp.concatenate(
-        [
-            jnp.concatenate(
-                [whole[at[i, j]] if i <= j else whole[at[j, i]].T for j in range(count)], axis=1
-            )
-            for i in range(count)
-        ],
-        axis=0,
-    )
     groups = lax.axis_size(("zh", "zl"))
-    precond = jnp.linalg.cholesky(gram, symmetrize_input=False).T / jnp.sqrt(jnp.float32(rows * groups))
-    slab = cols // groups
-    start = lax.axis_index(("zh", "zl")) * slab
-    return sketch, lax.dynamic_slice_in_dim(precond, start, slab, 0)
+    slab = lax.axis_index(("zh", "zl")).astype(jnp.int32)
+    precond = factor_rows(slab, whole, cols // groups, cols, 1.0 / math.sqrt(rows * groups))
+    return sketch, precond
 
 
 def solution(mesh):

time: 211 us -> 137 us (0.65)
  other arithmetic: 83.5 us -> 0.33 us
  Pallas kernels: 0 us -> 19.6 us
  local copies, waits for them, and re-layouts: 7.13 us -> 3.25 us
  matrix products: 9.9 us -> 6.06 us
  between operations: 3.63 us -> 0.82 us
    another operation x14 -> x0, other arithmetic: 83 us -> none  [per_device(): jnp.linalg.cholesky(gram, symmetrize_input=False)]
    pallas_call x0 -> x1, Pallas kernels: none -> 19.6 us  [factor_rows(): pl.pallas_call(functools.partial(factor_kernel, count=cols // TILE, scale...]
    another operation x6 -> x0, matrix products: 3.84 us -> none  [per_device(): jnp.linalg.cholesky(gram, symmetrize_input=False)]
    another operation x5 -> x0, local copies, waits for them, and re-layouts: 3.34 us -> none  [per_device(): jnp.linalg.cholesky(gram, symmetrize_input=False)]
where the time goes in v2:
time: 137 us; the launch traced here: 136 us
  blocking collectives  75.4 us (55%)
  Pallas kernels  19.6 us (14%)
  waiting for transfers between devices  15.7 us (11%)
  starting transfers between devices  15.2 us (11%)
  matrix products  6.06 us (4%)
  local copies, waits for them, and re-layouts  3.25 us (2%)
    all_to_all x4, blocking collectives, exchange(): return lax.all_to_all(value, axes, split_axis=0, concat_axis=0, tiled=True)  75.4 us
    pallas_call x1, Pallas kernels, factor_rows(): pl.pallas_call(functools.partial(factor_kernel, count=cols // TILE, scale...  19.6 us
    all_to_all x1, waiting for transfers between devices, exchange(): return lax.all_to_all(value, axes, split_axis=0, concat_axis=0, tiled=True)  12.8 us
    ppermute x1, starting transfers between devices, per_device(): from_pair = lax.ppermute(theirs, 'core', [(0, 1), (1, 0)])  8.81 us
    all_to_all x1, starting transfers between devices, exchange(): return lax.all_to_all(value, axes, split_axis=0, concat_axis=0, tiled=True)  6.38 us
    dot_general x2, matrix products, bucket_sums(): return jnp.dot(table, design, preferred_element_type=jnp.float32)  5.03 us
    ppermute x1, waiting for transfers between devices, per_device(): from_pair = lax.ppermute(theirs, 'core', [(0, 1), (1, 0)])  2.98 us
  transfers between devices with their start and end apart: 2, of which 2 were waited for; matrix products, arithmetic and copies ran while one was open for 0% of the time, Pallas kernels for 0%

profile of v2, /device:TPU:1, one launch (start us, length us, event | category | flops | bytes accessed | tf_op | source)
XLA Modules:
  0.0 136.4 jit_solution(3751751688891135156)
XLA Ops:
  0.6 0.0 copy-start
  0.7 0.1 iota_add_fusion
  0.7 0.1 add.47
  0.8 1.2 copy-done
  2.0 0.0 copy-start.3
  2.0 0.0 copy-start.4
  2.0 2.2 %fusion.1 = f32[768,512]{1,0:T(8,128)S(1)} fusion(bf16[1536,512]{1,0:T(8,128)(2,1)S(1)} %copy-done, s32[1536]{0:T(1024)} %param.5, s32[768]{0:T(1024)S(1)} %add.47, bf16[1536]{0:T(1024)(128)(2,1)} %param.4), kind=kOutput, calls=%fused_computation.3 | convolution fusion | flops 1210318848 | bytes 3158016 | tf_op jit(solution)/shard_map/dot_general | solution.py:45
  4.2 8.8 %collective-permute-start = (f32[768,512]{1,0:T(8,128)S(1)}, f32[768,512]{1,0:T(8,128)}, u32[]{:S(2)}, u32[]{:S(2)}) collective-permute-start(f32[768,512]{1,0:T(8,128)S(1)} %fusion.1), channel_id=1, source_target_pairs={{0,1},{1,0},{2,3},{3,2},{4,5},{5,4},{6,7},{7,6},{8,9},{9,8},{10,11... | collective-permute-start | bytes 4718600 | tf_op jit(solution)/shard_map/ppermute | solution.py:159
  13.1 0.1 iota_add_fusion.1
  13.2 0.1 add.43
  13.2 3.0 %collective-permute-done = f32[768,512]{1,0:T(8,128)} collective-permute-done((f32[768,512]{1,0:T(8,128)S(1)}, f32[768,512]{1,0:T(8,128)}, u32[]{:S(2)}, u32[]{:S(2)}) %collective-permute-start) | collective-permute-done | bytes 1572896 | tf_op jit(solution)/shard_map/ppermute | solution.py:159
  16.2 0.0 copy-done.3
  16.2 0.0 copy-done.4
  16.2 2.8 %fusion.6 = f32[768,512]{1,0:T(8,128)S(1)} fusion(f32[768,512]{1,0:T(8,128)} %collective-permute-done, bf16[1536,512]{1,0:T(8,128)(2,1)S(1)} %copy-done, s32[1536]{0:T(1024)S(1)} %copy-done.3, s32[768]{0:T(1024)S(1)} %add.43, bf16[1536]{0:T(1024)(128)(2,1)S(1)} %copy-done.4), kind=kOutput, calls=%fused_computation.8 | convolution fusion | flops 1210712064 | bytes 4730880 | tf_op jit(solution)/shard_map/dot_general | solution.py:45
  19.1 24.1 %all_to_all.25 = f32[16,48,512]{2,1,0:T(8,128)S(1)} all-to-all(f32[16,48,512]{2,1,0:T(8,128)S(1)} %bitcast.49), channel_id=1, replica_groups=mesh['zh'=4,'zl'=4,'x'=4,'y'=4,'core'=2] {'x','y'}, dimensions={0} | all-to-all | bytes 3145728 | tf_op jit(solution)/shard_map/all_to_all | solution.py:23
  43.2 0.1 reduce_sum.36
  43.3 0.0 copy-start.2
  43.3 1.0 fusion.25
  44.5 18.4 %all_to_all.26 = f32[32,40,128]{2,1,0:T(8,128)S(1)} all-to-all(f32[32,40,128]{2,1,0:T(8,128)S(1)} %bitcast.50), channel_id=1, replica_groups=mesh['zh'=4,'zl'=4,'x'=4,'y'=4,'core'=2] {'x','y','core'}, dimensions={0} | all-to-all | bytes 1310720 | tf_op jit(solution)/shard_map/all_to_all | solution.py:23
  63.0 0.0 copy-done.2
  63.0 0.1 reduce_sum.37
  63.0 8.7 %all_to_all.27 = f32[4,40,128]{2,1,0:T(8,128)S(1)} all-to-all(f32[4,40,128]{2,1,0:T(8,128)S(1)} %broadcast_in_dim.40), channel_id=1, replica_groups=mesh['zh'=4,'zl'=4,'x'=4,'y'=4,'core'=2] {'zl'}, dimensions={0} | all-to-all | bytes 163840 | tf_op jit(solution)/shard_map/all_to_all | solution.py:23
  71.7 24.2 %all_to_all.28 = f32[4,40,128]{2,1,0:T(8,128)S(1)} all-to-all(f32[4,40,128]{2,1,0:T(8,128)S(1)} %broadcast_in_dim.41), channel_id=1, replica_groups=mesh['zh'=4,'zl'=4,'x'=4,'y'=4,'core'=2] {'zh'}, dimensions={0} | all-to-all | bytes 163840 | tf_op jit(solution)/shard_map/all_to_all | solution.py:23
  95.9 0.9 broadcast_in_dim.42
  96.8 6.4 %all-to-all-start.4 = ((f32[32,40,128]{2,1,0:T(8,128)}), f32[32,40,128]{2,1,0:T(8,128)S(1)}, u32[]{:S(2)}, u32[]{:S(2)}) async-start(f32[32,40,128]{2,1,0:T(8,128)} %broadcast_in_dim.42), calls=%async_computation.4 | async-start | bytes 1310720 | tf_op jit(solution)/shard_map/all_to_all | solution.py:23
  103.2 12.8 %all-to-all-done.4 = f32[32,40,128]{2,1,0:T(8,128)S(1)} async-done(((f32[32,40,128]{2,1,0:T(8,128)}), f32[32,40,128]{2,1,0:T(8,128)S(1)}, u32[]{:S(2)}, u32[]{:S(2)}) %all-to-all-start.4) | async-done | bytes 655392 | tf_op jit(solution)/shard_map/all_to_all | solution.py:23
  116.0 0.0 copy-start.1
  116.0 0.8 copy-done.1
  116.8 19.6 %factor_rows.1 = f32[32,512]{1,0:T(8,128)} custom-call(s32[1]{0:T(128)} %bitcast.1.slab_ref, f32[10,128,128]{2,1,0:T(8,128)} %bitcast.48), custom_call_target="tpu_custom_call" | custom-call | tf_op jit(solution)/shard_map/factor_rows/pallas_call | solution.py:143
  (16 shorter events, 0.2 us)
Async XLA Ops:
  0.6 1.4 %copy-start = (bf16[1536,512]{1,0:T(8,128)(2,1)S(1)}, bf16[1536,512]{1,0:T(8,128)(2,1)}, u32[]{:S(2)}) copy-start(bf16[1536,512]{1,0:T(8,128)(2,1)} %param.3) | copy-start | bytes 4718596
  2.0 14.2 %copy-start.3 = (s32[1536]{0:T(1024)S(1)}, s32[1536]{0:T(1024)}, u32[]{:S(2)}) copy-start(s32[1536]{0:T(1024)} %param.5) | copy-start | bytes 18436
  2.0 14.2 %copy-start.4 = (bf16[1536]{0:T(1024)(128)(2,1)S(1)}, bf16[1536]{0:T(1024)(128)(2,1)}, u32[]{:S(2)}) copy-start(bf16[1536]{0:T(1024)(128)(2,1)} %param.4) | copy-start | bytes 9220
  4.2 12.0 %collective-permute-start = (f32[768,512]{1,0:T(8,128)S(1)}, f32[768,512]{1,0:T(8,128)}, u32[]{:S(2)}, u32[]{:S(2)}) collective-permute-start(f32[768,512]{1,0:T(8,128)S(1)} %fusion.1), channel_id=1, source_target_pairs={{0,1},{1,0},{2,3},{3,2},{4,5},{5,4},{6,7},{7,6},{8,9},{9,8},{10,11... | collective-permute-start | bytes 4718600 | tf_op jit(solution)/shard_map/ppermute | solution.py:159
  43.3 19.7 %copy-start.2 = (f32[48,512]{1,0:T(8,128)}, f32[48,512]{1,0:T(8,128)S(1)}, u32[]{:S(2)}) copy-start(f32[48,512]{1,0:T(8,128)S(1)} %reduce_sum.36) | copy-start | bytes 294916
  96.8 19.1 %all-to-all-start.4 = ((f32[32,40,128]{2,1,0:T(8,128)}), f32[32,40,128]{2,1,0:T(8,128)S(1)}, u32[]{:S(2)}, u32[]{:S(2)}) async-start(f32[32,40,128]{2,1,0:T(8,128)} %broadcast_in_dim.42), calls=%async_computation.4 | async-start | bytes 1310720 | tf_op jit(solution)/shard_map/all_to_all | solution.py:23
  116.0 0.8 copy-start.1

commit v3 on v2

--- a/solution.py
+++ b/solution.py
@@ -64,19 +64,21 @@
     return jnp.broadcast_to(value, (SUB, TILE))
 
 
+def pivots_of(rows, left):
+    return {(t, u): fill(rows[t][:, left + u : left + u + 1]) for t in range(SUB) for u in range(t, SUB)}
+
+
 def factor_kernel(slab_ref, gram_ref, out_ref, work, *, count, scale):
     at = {pair: n for n, pair in enumerate(blocks_of(count * TILE))}
     work[...] = gram_ref[...]
     for b in range(count):
         js = range(b, count)
-        ahead = None
+        ahead = ready = None
         for top in range(0, TILE, SUB):
-            rows = ahead
+            rows, pivot = ahead, ready
             if rows is None:
                 rows = [{j: fill(work[at[b, j], top + t : top + t + 1, :]) for j in js} for t in range(SUB)]
-            pivot = {
-                (t, u): fill(rows[t][b][:, top + u : top + u + 1]) for t in range(SUB) for u in range(t, SUB)
-            }
+                pivot = pivots_of([row[b] for row in rows], top)
             done = []
             for t in range(SUB):
                 inverse = lax.rsqrt(pivot[t, t])
@@ -91,17 +93,22 @@
             for t in range(SUB):
                 for j in js:
                     work[at[b, j], top + t : top + t + 1, :] = done[t][j][0:1, :]
-            ahead = None
+            ahead = ready = None
             below = top + SUB
             if below < TILE:
                 ahead = [
                     {j: fill(work[at[b, j], below + u : below + u + 1, :]) for j in js} for u in range(SUB)
                 ]
                 for t in range(SUB):
+                    if t == SUB // 2:
+                        ready = pivots_of([row[b] for row in ahead], below)
+                    coef = [fill(done[t][b][:, below + u : below + u + 1]) for u in range(SUB)]
+                    if ready is not None:
+                        for u, v in ready:
+                            ready[u, v] = ready[u, v] - coef[u] * coef[v]
                     for u in range(SUB):
-                        coef = fill(done[t][b][:, below + u : below + u + 1])
                         for j in js:
-                            ahead[u][j] = ahead[u][j] - coef * done[t][j]
+                            ahead[u][j] = ahead[u][j] - coef[u] * done[t][j]
             later = top + 2 * SUB
             if later < TILE:
                 left = work[at[b, b], top : top + SUB, :]
@@ -147,7 +154,7 @@
         out_specs=pl.BlockSpec(memory_space=pltpu.VMEM),
         scratch_shapes=[pltpu.VMEM(packed.shape, jnp.float32)],
         name="factor_rows",
-    )(slab.reshape(1), packed)
+    )(slab.reshape(1), pltpu.with_memory_space_constraint(packed, pltpu.VMEM))
 
 
 def per_device(design, scales, buckets):
@@ -155,9 +162,11 @@
     chips = lax.axis_size(("x", "y"))
     owned = rows // (2 * chips)
     core = lax.axis_index("core")
+    slab = lax.axis_index(("zh", "zl")).astype(jnp.int32)
+    core, slab, buckets = lax.optimization_barrier((core, slab, buckets))
     theirs = bucket_sums(design, scales, buckets, 1 - core, chips, owned)
     from_pair = lax.ppermute(theirs, "core", [(0, 1), (1, 0)])
-    ours = bucket_sums(design, scales, buckets, core, chips, owned)
+    ours = lax.optimization_barrier(bucket_sums(design, scales, buckets, core, chips, owned))
     paired = (ours + from_pair).reshape(chips, owned, cols)
     sketch = jnp.sum(exchange(paired, ("x", "y")), axis=0)
     local = self_gram(sketch)
@@ -168,11 +177,10 @@
     devices = 2 * chips
     packed = packed.reshape(devices, -1, TILE)
     piece = jnp.sum(exchange(packed, ("x", "y", "core")), axis=0)
+    piece = jnp.sum(spread(piece, ("zh",)), axis=0)
     piece = jnp.sum(spread(piece, ("zl",)), axis=0)
-    piece = jnp.sum(spread(piece, ("zh",)), axis=0)
     whole = spread(piece, ("x", "y", "core")).reshape(len(pairs), TILE, TILE)
     groups = lax.axis_size(("zh", "zl"))
-    slab = lax.axis_index(("zh", "zl")).astype(jnp.int32)
     precond = factor_rows(slab, whole, cols // groups, cols, 1.0 / math.sqrt(rows * groups))
     return sketch, precond
 

time: 137 us -> 132 us (0.964)
  blocking collectives: 75.4 us -> 95.2 us
  waiting for transfers between devices: 15.7 us -> 1.62 us
  starting transfers between devices: 15.2 us -> 8.79 us
  Pallas kernels: 19.6 us -> 17.5 us
  local copies, waits for them, and re-layouts: 3.25 us -> 1.57 us
    all_to_all x4 -> x5, blocking collectives: 75.4 us -> 95.2 us  [exchange(): return lax.all_to_all(value, axes, split_axis=0, concat_axis=0, tiled=True)]
    all_to_all x1 -> x0, waiting for transfers between devices: 12.8 us -> none  [exchange(): return lax.all_to_all(value, axes, split_axis=0, concat_axis=0, tiled=True)]
    all_to_all x1 -> x0, starting transfers between devices: 6.38 us -> none  [exchange(): return lax.all_to_all(value, axes, split_axis=0, concat_axis=0, tiled=True)]
    pallas_call x1, Pallas kernels: 19.6 us -> 17.5 us  [factor_rows(): pl.pallas_call(functools.partial(factor_kernel, count=cols // TILE, scale...]
  transfers between devices with their start and end apart: 2 -> 1, of which waited for: 2 -> 1; matrix products, arithmetic and copies ran while one was open for 0% -> 1% of each run, Pallas kernels for 0% -> 0%
where the time goes in v3:
time: 132 us
  blocking collectives  95.2 us (72%)
  Pallas kernels  17.5 us (13%)
  starting transfers between devices  8.79 us (7%)
  matrix products  5.81 us (4%)
  waiting for transfers between devices  1.62 us (1%)
  local copies, waits for them, and re-layouts  1.57 us (1%)
    all_to_all x5, blocking collectives, exchange(): return lax.all_to_all(value, axes, split_axis=0, concat_axis=0, tiled=True)  95.2 us
    pallas_call x1, Pallas kernels, factor_rows(): pl.pallas_call(functools.partial(factor_kernel, count=cols // TILE, scale...  17.5 us
    ppermute x1, starting transfers between devices, per_device(): from_pair = lax.ppermute(theirs, 'core', [(0, 1), (1, 0)])  8.79 us
    dot_general x2, matrix products, bucket_sums(): return jnp.dot(table, design, preferred_element_type=jnp.float32)  4.78 us
  transfers between devices with their start and end apart: 1, of which 1 were waited for; matrix products, arithmetic and copies ran while one was open for 1% of the time, Pallas kernels for 0%

profile of v3, /device:TPU:1, one launch (start us, length us, event | category | flops | bytes accessed | tf_op | source)
XLA Modules:
  0.0 131.9 jit_solution(3659351902792600459)
XLA Ops:
  0.6 0.0 copy-start
  0.7 0.1 iota_add_fusion
  0.7 0.1 add.48
  0.8 1.2 copy-done
  2.0 0.0 copy-start.2
  2.0 0.0 copy-start.3
  2.0 3.4 %fusion.1 = f32[768,512]{1,0:T(8,128)} fusion(bf16[1536,512]{1,0:T(8,128)(2,1)S(1)} %copy-done, s32[1536]{0:T(1024)} %param.5, s32[768]{0:T(1024)S(1)} %add.48, bf16[1536]{0:T(1024)(128)(2,1)} %param.4), kind=kOutput, calls=%fused_computation.3 | convolution fusion | flops 1210318848 | bytes 3158016 | tf_op jit(solution)/shard_map/dot_general | solution.py:45
  5.4 8.8 %collective-permute-start = (f32[768,512]{1,0:T(8,128)}, f32[768,512]{1,0:T(8,128)S(1)}, u32[]{:S(2)}, u32[]{:S(2)}) collective-permute-start(f32[768,512]{1,0:T(8,128)} %fusion.1), channel_id=1, source_target_pairs={{0,1},{1,0},{2,3},{3,2},{4,5},{5,4},{6,7},{7,6},{8,9},{9,8},{10,11... | collective-permute-start | bytes 4718600 | tf_op jit(solution)/shard_map/ppermute | solution.py:168
  14.2 0.1 iota_add_fusion.1
  14.3 0.1 add.44
  14.4 0.0 copy-done.2
  14.4 0.0 copy-done.3
  14.4 1.4 %fusion = f32[768,512]{1,0:T(8,128)S(1)} fusion(bf16[1536,512]{1,0:T(8,128)(2,1)S(1)} %copy-done, s32[1536]{0:T(1024)S(1)} %copy-done.2, s32[768]{0:T(1024)S(1)} %add.44, bf16[1536]{0:T(1024)(128)(2,1)S(1)} %copy-done.3), kind=kOutput, calls=%fused_computation.2 | convolution fusion | flops 1210318848 | bytes 3158016 | tf_op jit(solution)/shard_map/dot_general | solution.py:45
  15.8 1.6 %collective-permute-done = f32[768,512]{1,0:T(8,128)S(1)} collective-permute-done((f32[768,512]{1,0:T(8,128)}, f32[768,512]{1,0:T(8,128)S(1)}, u32[]{:S(2)}, u32[]{:S(2)}) %collective-permute-start) | collective-permute-done | bytes 1572896 | tf_op jit(solution)/shard_map/ppermute | solution.py:168
  17.4 0.3 add.49
  17.8 24.1 %all_to_all.25 = f32[16,48,512]{2,1,0:T(8,128)S(1)} all-to-all(f32[16,48,512]{2,1,0:T(8,128)S(1)} %bitcast.49), channel_id=1, replica_groups=mesh['zh'=4,'zl'=4,'x'=4,'y'=4,'core'=2] {'x','y'}, dimensions={0} | all-to-all | bytes 3145728 | tf_op jit(solution)/shard_map/all_to_all | solution.py:23
  41.9 0.1 reduce_sum.36
  42.0 0.0 copy-start.1
  42.0 1.0 fusion.24
  43.2 18.4 %all_to_all.26 = f32[32,40,128]{2,1,0:T(8,128)S(1)} all-to-all(f32[32,40,128]{2,1,0:T(8,128)S(1)} %bitcast.50), channel_id=1, replica_groups=mesh['zh'=4,'zl'=4,'x'=4,'y'=4,'core'=2] {'x','y','core'}, dimensions={0} | all-to-all | bytes 1310720 | tf_op jit(solution)/shard_map/all_to_all | solution.py:23
  61.7 0.0 copy-done.1
  61.7 0.1 reduce_sum.37
  61.7 25.3 %all_to_all.27 = f32[4,40,128]{2,1,0:T(8,128)S(1)} all-to-all(f32[4,40,128]{2,1,0:T(8,128)S(1)} %broadcast_in_dim.40), channel_id=1, replica_groups=mesh['zh'=4,'zl'=4,'x'=4,'y'=4,'core'=2] {'zh'}, dimensions={0} | all-to-all | bytes 163840 | tf_op jit(solution)/shard_map/all_to_all | solution.py:23
  87.0 7.3 %all_to_all.28 = f32[4,40,128]{2,1,0:T(8,128)S(1)} all-to-all(f32[4,40,128]{2,1,0:T(8,128)S(1)} %broadcast_in_dim.41), channel_id=1, replica_groups=mesh['zh'=4,'zl'=4,'x'=4,'y'=4,'core'=2] {'zl'}, dimensions={0} | all-to-all | bytes 163840 | tf_op jit(solution)/shard_map/all_to_all | solution.py:23
  94.4 20.0 %all_to_all.29 = f32[32,40,128]{2,1,0:T(8,128)S(1)} all-to-all(f32[32,40,128]{2,1,0:T(8,128)S(1)} %broadcast_in_dim.42), channel_id=1, replica_groups=mesh['zh'=4,'zl'=4,'x'=4,'y'=4,'core'=2] {'x','y','core'}, dimensions={0} | all-to-all | bytes 1310720 | tf_op jit(solution)/shard_map/all_to_all | solution.py:23
  114.4 17.5 %factor_rows.1 = f32[32,512]{1,0:T(8,128)} custom-call(s32[1]{0:T(128)} %bitcast.1.slab_ref, f32[10,128,128]{2,1,0:T(8,128)S(1)} %bitcast.48), custom_call_target="tpu_custom_call" | custom-call | tf_op jit(solution)/shard_map/factor_rows/pallas_call | solution.py:150
  (17 shorter events, 0.2 us)
Async XLA Ops:
  0.6 1.4 %copy-start = (bf16[1536,512]{1,0:T(8,128)(2,1)S(1)}, bf16[1536,512]{1,0:T(8,128)(2,1)}, u32[]{:S(2)}) copy-start(bf16[1536,512]{1,0:T(8,128)(2,1)} %param.3) | copy-start | bytes 4718596
  2.0 12.3 %copy-start.2 = (s32[1536]{0:T(1024)S(1)}, s32[1536]{0:T(1024)}, u32[]{:S(2)}) copy-start(s32[1536]{0:T(1024)} %param.5) | copy-start | bytes 18436
  2.0 12.3 %copy-start.3 = (bf16[1536]{0:T(1024)(128)(2,1)S(1)}, bf16[1536]{0:T(1024)(128)(2,1)}, u32[]{:S(2)}) copy-start(bf16[1536]{0:T(1024)(128)(2,1)} %param.4) | copy-start | bytes 9220
  5.4 12.0 %collective-permute-start = (f32[768,512]{1,0:T(8,128)}, f32[768,512]{1,0:T(8,128)S(1)}, u32[]{:S(2)}, u32[]{:S(2)}) collective-permute-start(f32[768,512]{1,0:T(8,128)} %fusion.1), channel_id=1, source_target_pairs={{0,1},{1,0},{2,3},{3,2},{4,5},{5,4},{6,7},{7,6},{8,9},{9,8},{10,11... | collective-permute-start | bytes 4718600 | tf_op jit(solution)/shard_map/ppermute | solution.py:168
  42.0 19.7 %copy-start.1 = (f32[48,512]{1,0:T(8,128)}, f32[48,512]{1,0:T(8,128)S(1)}, u32[]{:S(2)}) copy-start(f32[48,512]{1,0:T(8,128)S(1)} %reduce_sum.36) | copy-start | bytes 294916

commit v4 on v3

--- a/solution.py
+++ b/solution.py
@@ -17,6 +17,24 @@
 def blocks_of(size):
     count = size // TILE
     return [(i, j) for i in range(count) for j in range(i, count)]
+
+
+def folded_of(size):
+    count = size // TILE
+    return [(i, i + 1) for i in range(0, count, 2)], [(i, j) for i in range(count) for j in range(i + 1, count)]
+
+
+def fold(gram, squares, devices):
+    block = lambda i, j: gram[i * TILE : (i + 1) * TILE, j * TILE : (j + 1) * TILE]
+    rows, lanes = (lax.broadcasted_iota(jnp.int32, (TILE, TILE), d) for d in (0, 1))
+    pairs, above = folded_of(gram.shape[0])
+    parts = [jnp.where(rows <= lanes, block(i, i), block(j, j)) for i, j in pairs]
+    parts += [block(i, j) for i, j in above]
+    parts += [squares[j * TILE : (j + 1) * TILE][None] for _, j in pairs]
+    height = sum(part.shape[0] for part in parts)
+    missing = -height % devices
+    parts.append(jnp.zeros((missing, TILE), jnp.float32))
+    return jnp.concatenate(parts, axis=0).reshape(devices, (height + missing) // devices, 1, TILE)
 
 
 def exchange(value, axes):
@@ -70,7 +88,17 @@
 
 def factor_kernel(slab_ref, gram_ref, out_ref, work, *, count, scale):
     at = {pair: n for n, pair in enumerate(blocks_of(count * TILE))}
-    work[...] = gram_ref[...]
+    pairs, above = folded_of(count * TILE)
+    shape = (TILE, TILE)
+    rows, lanes = lax.broadcasted_iota(jnp.int32, shape, 0), lax.broadcasted_iota(jnp.int32, shape, 1)
+    last = (len(pairs) + len(above)) * TILE
+    for n, (i, j) in enumerate(pairs):
+        both = gram_ref[n * TILE : (n + 1) * TILE, :]
+        work[at[i, i]] = both
+        diagonal = jnp.broadcast_to(gram_ref[last + n : last + n + 1, :], shape)
+        work[at[j, j]] = jnp.where(rows == lanes, diagonal, both.T)
+    for n, pair in enumerate(above, len(pairs)):
+        work[at[pair]] = gram_ref[n * TILE : (n + 1) * TILE, :]
     for b in range(count):
         js = range(b, count)
         ahead = ready = None
@@ -152,7 +180,7 @@
         out_shape=jax.ShapeDtypeStruct((height, cols), jnp.float32),
         in_specs=[pl.BlockSpec(memory_space=pltpu.SMEM), pl.BlockSpec(memory_space=pltpu.VMEM)],
         out_specs=pl.BlockSpec(memory_space=pltpu.VMEM),
-        scratch_shapes=[pltpu.VMEM(packed.shape, jnp.float32)],
+        scratch_shapes=[pltpu.VMEM((len(blocks_of(cols)), TILE, TILE), jnp.float32)],
         name="factor_rows",
     )(slab.reshape(1), pltpu.with_memory_space_constraint(packed, pltpu.VMEM))
 
@@ -170,16 +198,11 @@
     paired = (ours + from_pair).reshape(chips, owned, cols)
     sketch = jnp.sum(exchange(paired, ("x", "y")), axis=0)
     local = self_gram(sketch)
-    pairs = blocks_of(cols)
-    packed = jnp.stack(
-        [local[i * TILE : (i + 1) * TILE, j * TILE : (j + 1) * TILE] for i, j in pairs]
-    )
-    devices = 2 * chips
-    packed = packed.reshape(devices, -1, TILE)
+    packed = fold(local, jnp.sum(sketch * sketch, axis=0), 2 * chips)
     piece = jnp.sum(exchange(packed, ("x", "y", "core")), axis=0)
     piece = jnp.sum(spread(piece, ("zh",)), axis=0)
     piece = jnp.sum(spread(piece, ("zl",)), axis=0)
-    whole = spread(piece, ("x", "y", "core")).reshape(len(pairs), TILE, TILE)
+    whole = spread(piece, ("x", "y", "core")).reshape(-1, TILE)
     groups = lax.axis_size(("zh", "zl"))
     precond = factor_rows(slab, whole, cols // groups, cols, 1.0 / math.sqrt(rows * groups))
     return sketch, precond

time: 132 us -> 130 us (0.985)
  blocking collectives: 95.2 us -> 92.2 us
    all_to_all x5, blocking collectives: 95.2 us -> 92.2 us  [exchange(): return lax.all_to_all(value, axes, split_axis=0, concat_axis=0, tiled=True)]
where the time goes in v4:
time: 130 us
  blocking collectives  92.2 us (71%)
  Pallas kernels  17.7 us (14%)
  starting transfers between devices  8.79 us (7%)
  matrix products  5.81 us (4%)
  local copies, waits for them, and re-layouts  1.99 us (2%)
  waiting for transfers between devices  1.62 us (1%)
    all_to_all x5, blocking collectives, exchange(): return lax.all_to_all(value, axes, split_axis=0, concat_axis=0, tiled=True)  92.2 us
    pallas_call x1, Pallas kernels, factor_rows(): pl.pallas_call(functools.partial(factor_kernel, count=cols // TILE, scale...  17.7 us
    ppermute x1, starting transfers between devices, per_device(): from_pair = lax.ppermute(theirs, 'core', [(0, 1), (1, 0)])  8.79 us
    dot_general x2, matrix products, bucket_sums(): return jnp.dot(table, design, preferred_element_type=jnp.float32)  4.78 us
  transfers between devices with their start and end apart: 1, of which 1 were waited for; matrix products, arithmetic and copies ran while one was open for 1% of the time, Pallas kernels for 0%

profile of v4, /device:TPU:1, one launch (start us, length us, event | category | flops | bytes accessed | tf_op | source)
XLA Modules:
  0.0 130.1 jit_solution(1107143328052945825)
XLA Ops:
  0.6 0.0 copy-start
  0.7 0.1 iota_add_fusion
  0.7 0.1 add.48
  0.8 1.2 copy-done
  2.0 0.0 copy-start.2
  2.0 0.0 copy-start.3
  2.0 3.4 %fusion.1 = f32[768,512]{1,0:T(8,128)} fusion(bf16[1536,512]{1,0:T(8,128)(2,1)S(1)} %copy-done, s32[1536]{0:T(1024)} %param.5, s32[768]{0:T(1024)S(1)} %add.48, bf16[1536]{0:T(1024)(128)(2,1)} %param.4), kind=kOutput, calls=%fused_computation.3 | convolution fusion | flops 1210318848 | bytes 3158016 | tf_op jit(solution)/shard_map/dot_general | solution.py:63
  5.4 8.8 %collective-permute-start = (f32[768,512]{1,0:T(8,128)}, f32[768,512]{1,0:T(8,128)S(1)}, u32[]{:S(2)}, u32[]{:S(2)}) collective-permute-start(f32[768,512]{1,0:T(8,128)} %fusion.1), channel_id=1, source_target_pairs={{0,1},{1,0},{2,3},{3,2},{4,5},{5,4},{6,7},{7,6},{8,9},{9,8},{10,11... | collective-permute-start | bytes 4718600 | tf_op jit(solution)/shard_map/ppermute | solution.py:196
  14.2 0.1 iota_add_fusion.1
  14.3 0.1 add.44
  14.4 0.0 copy-done.2
  14.4 0.0 copy-done.3
  14.4 1.4 %fusion = f32[768,512]{1,0:T(8,128)S(1)} fusion(bf16[1536,512]{1,0:T(8,128)(2,1)S(1)} %copy-done, s32[1536]{0:T(1024)S(1)} %copy-done.2, s32[768]{0:T(1024)S(1)} %add.44, bf16[1536]{0:T(1024)(128)(2,1)S(1)} %copy-done.3), kind=kOutput, calls=%fused_computation.2 | convolution fusion | flops 1210318848 | bytes 3158016 | tf_op jit(solution)/shard_map/dot_general | solution.py:63
  15.8 1.6 %collective-permute-done = f32[768,512]{1,0:T(8,128)S(1)} collective-permute-done((f32[768,512]{1,0:T(8,128)}, f32[768,512]{1,0:T(8,128)S(1)}, u32[]{:S(2)}, u32[]{:S(2)}) %collective-permute-start) | collective-permute-done | bytes 1572896 | tf_op jit(solution)/shard_map/ppermute | solution.py:196
  17.4 0.3 add.49
  17.8 24.1 %all_to_all.25 = f32[16,48,512]{2,1,0:T(8,128)S(1)} all-to-all(f32[16,48,512]{2,1,0:T(8,128)S(1)} %bitcast.13), channel_id=1, replica_groups=mesh['zh'=4,'zl'=4,'x'=4,'y'=4,'core'=2] {'x','y'}, dimensions={0} | all-to-all | bytes 3145728 | tf_op jit(solution)/shard_map/all_to_all | solution.py:41
  41.9 0.1 reduce_sum.45
  42.0 0.0 copy-start.1
  42.0 1.0 fusion.15
  43.2 0.2 concatenate.4
  43.4 0.0 copy-done.1
  43.4 17.3 %all_to_all.26 = f32[32,33,1,128]{3,2,1,0:T(1,128)S(1)} all-to-all(f32[32,33,1,128]{3,2,1,0:T(1,128)S(1)} %bitcast.14), channel_id=1, replica_groups=mesh['zh'=4,'zl'=4,'x'=4,'y'=4,'core'=2] {'x','y','core'}, dimensions={0} | all-to-all | bytes 1081344 | tf_op jit(solution)/shard_map/all_to_all | solution.py:41
  60.7 0.3 reduce_sum.47
  61.0 24.9 %all_to_all.27 = f32[4,33,1,128]{3,2,1,0:T(1,128)S(1)} all-to-all(f32[4,33,1,128]{3,2,1,0:T(1,128)S(1)} %broadcast_in_dim.52), channel_id=1, replica_groups=mesh['zh'=4,'zl'=4,'x'=4,'y'=4,'core'=2] {'zh'}, dimensions={0} | all-to-all | bytes 135168 | tf_op jit(solution)/shard_map/all_to_all | solution.py:41
  85.9 0.1 reduce_sum.48
  86.0 7.3 %all_to_all.28 = f32[4,33,1,128]{3,2,1,0:T(1,128)S(1)} all-to-all(f32[4,33,1,128]{3,2,1,0:T(1,128)S(1)} %broadcast_in_dim.53), channel_id=1, replica_groups=mesh['zh'=4,'zl'=4,'x'=4,'y'=4,'core'=2] {'zl'}, dimensions={0} | all-to-all | bytes 135168 | tf_op jit(solution)/shard_map/all_to_all | solution.py:41
  93.4 0.1 reduce_sum.49
  93.4 0.3 broadcast_in_dim.54
  93.7 18.6 %all_to_all.29 = f32[32,33,1,128]{3,2,1,0:T(1,128)S(1)} all-to-all(f32[32,33,1,128]{3,2,1,0:T(1,128)S(1)} %broadcast_in_dim.54), channel_id=1, replica_groups=mesh['zh'=4,'zl'=4,'x'=4,'y'=4,'core'=2] {'x','y','core'}, dimensions={0} | all-to-all | bytes 1081344 | tf_op jit(solution)/shard_map/all_to_all | solution.py:41
  112.4 17.7 %factor_rows.1 = f32[32,512]{1,0:T(8,128)} custom-call(s32[1]{0:T(128)} %bitcast.1.slab_ref, f32[1056,128]{1,0:T(8,128)S(1)} %bitcast.12), custom_call_target="tpu_custom_call" | custom-call | tf_op jit(solution)/shard_map/factor_rows/pallas_call | solution.py:178
  (9 shorter events, 0.2 us)
Async XLA Ops:
  0.6 1.4 %copy-start = (bf16[1536,512]{1,0:T(8,128)(2,1)S(1)}, bf16[1536,512]{1,0:T(8,128)(2,1)}, u32[]{:S(2)}) copy-start(bf16[1536,512]{1,0:T(8,128)(2,1)} %param.3) | copy-start | bytes 4718596
  2.0 12.3 %copy-start.2 = (s32[1536]{0:T(1024)S(1)}, s32[1536]{0:T(1024)}, u32[]{:S(2)}) copy-start(s32[1536]{0:T(1024)} %param.5) | copy-start | bytes 18436
  2.0 12.3 %copy-start.3 = (bf16[1536]{0:T(1024)(128)(2,1)S(1)}, bf16[1536]{0:T(1024)(128)(2,1)}, u32[]{:S(2)}) copy-start(bf16[1536]{0:T(1024)(128)(2,1)} %param.4) | copy-start | bytes 9220
  5.4 12.0 %collective-permute-start = (f32[768,512]{1,0:T(8,128)}, f32[768,512]{1,0:T(8,128)S(1)}, u32[]{:S(2)}, u32[]{:S(2)}) collective-permute-start(f32[768,512]{1,0:T(8,128)} %fusion.1), channel_id=1, source_target_pairs={{0,1},{1,0},{2,3},{3,2},{4,5},{5,4},{6,7},{7,6},{8,9},{9,8},{10,11... | collective-permute-start | bytes 4718600 | tf_op jit(solution)/shard_map/ppermute | solution.py:196
  42.0 1.4 %copy-start.1 = (f32[48,512]{1,0:T(8,128)}, f32[48,512]{1,0:T(8,128)S(1)}, u32[]{:S(2)}) copy-start(f32[48,512]{1,0:T(8,128)S(1)} %reduce_sum.45) | copy-start | bytes 294916

commit v5 on v4

--- a/solution.py
+++ b/solution.py
@@ -47,13 +47,13 @@
 
 
 def self_gram(matrix):
-    return lax.dot_general(
-        matrix,
-        matrix,
-        (((0,), (0,)), ((), ())),
-        precision=lax.Precision.HIGHEST,
-        preferred_element_type=jnp.float32,
-    )
+    high = lax.reduce_precision(matrix, 8, 7)
+    rest = matrix - high
+    middle = lax.reduce_precision(rest, 8, 7)
+    low = rest - middle
+    tall = jnp.concatenate([high, high, middle, middle, high, low]).astype(jnp.bfloat16)
+    wide = jnp.concatenate([high, middle, high, middle, low, high]).astype(jnp.bfloat16)
+    return lax.dot_general(tall, wide, (((0,), (0,)), ((), ())), preferred_element_type=jnp.float32)
 
 
 def bucket_sums(design, scales, buckets, core, chips, owned):

time: 130 us -> 130 us (level)
  no operation moved by 1% of the time
where the time goes in v5:
time: 130 us
  blocking collectives  92.2 us (71%)
  Pallas kernels  17.7 us (14%)
  starting transfers between devices  8.79 us (7%)
  matrix products  5.24 us (4%)
  local copies, waits for them, and re-layouts  2.05 us (2%)
  waiting for transfers between devices  1.62 us (1%)
    all_to_all x5, blocking collectives, exchange(): return lax.all_to_all(value, axes, split_axis=0, concat_axis=0, tiled=True)  92.2 us
    pallas_call x1, Pallas kernels, factor_rows(): pl.pallas_call(functools.partial(factor_kernel, count=cols // TILE, scale...  17.7 us
    ppermute x1, starting transfers between devices, per_device(): from_pair = lax.ppermute(theirs, 'core', [(0, 1), (1, 0)])  8.79 us
    dot_general x2, matrix products, bucket_sums(): return jnp.dot(table, design, preferred_element_type=jnp.float32)  4.78 us
  transfers between devices with their start and end apart: 1, of which 1 were waited for; matrix products, arithmetic and copies ran while one was open for 1% of the time, Pallas kernels for 0%

profile of v5, /device:TPU:1, one launch (start us, length us, event | category | flops | bytes accessed | tf_op | source)
XLA Modules:
  0.0 129.7 jit_solution(11997072956230056061)
XLA Ops:
  0.6 0.0 copy-start
  0.7 0.1 iota_add_fusion
  0.7 0.1 add.48
  0.8 1.2 copy-done
  2.0 0.0 copy-start.2
  2.0 0.0 copy-start.3
  2.0 3.4 %fusion.1 = f32[768,512]{1,0:T(8,128)} fusion(bf16[1536,512]{1,0:T(8,128)(2,1)S(1)} %copy-done, s32[1536]{0:T(1024)} %param.5, s32[768]{0:T(1024)S(1)} %add.48, bf16[1536]{0:T(1024)(128)(2,1)} %param.4), kind=kOutput, calls=%fused_computation.3 | convolution fusion | flops 1210318848 | bytes 3158016 | tf_op jit(solution)/shard_map/dot_general | solution.py:63
  5.4 8.8 %collective-permute-start = (f32[768,512]{1,0:T(8,128)}, f32[768,512]{1,0:T(8,128)S(1)}, u32[]{:S(2)}, u32[]{:S(2)}) collective-permute-start(f32[768,512]{1,0:T(8,128)} %fusion.1), channel_id=1, source_target_pairs={{0,1},{1,0},{2,3},{3,2},{4,5},{5,4},{6,7},{7,6},{8,9},{9,8},{10,11... | collective-permute-start | bytes 4718600 | tf_op jit(solution)/shard_map/ppermute | solution.py:196
  14.2 0.1 iota_add_fusion.1
  14.3 0.1 add.44
  14.4 0.0 copy-done.2
  14.4 0.0 copy-done.3
  14.4 1.4 %fusion = f32[768,512]{1,0:T(8,128)S(1)} fusion(bf16[1536,512]{1,0:T(8,128)(2,1)S(1)} %copy-done, s32[1536]{0:T(1024)S(1)} %copy-done.2, s32[768]{0:T(1024)S(1)} %add.44, bf16[1536]{0:T(1024)(128)(2,1)S(1)} %copy-done.3), kind=kOutput, calls=%fused_computation.2 | convolution fusion | flops 1210318848 | bytes 3158016 | tf_op jit(solution)/shard_map/dot_general | solution.py:63
  15.8 1.6 %collective-permute-done = f32[768,512]{1,0:T(8,128)S(1)} collective-permute-done((f32[768,512]{1,0:T(8,128)}, f32[768,512]{1,0:T(8,128)S(1)}, u32[]{:S(2)}, u32[]{:S(2)}) %collective-permute-start) | collective-permute-done | bytes 1572896 | tf_op jit(solution)/shard_map/ppermute | solution.py:196
  17.4 0.3 add.49
  17.8 24.1 %all_to_all.25 = f32[16,48,512]{2,1,0:T(8,128)S(1)} all-to-all(f32[16,48,512]{2,1,0:T(8,128)S(1)} %bitcast.13), channel_id=1, replica_groups=mesh['zh'=4,'zl'=4,'x'=4,'y'=4,'core'=2] {'x','y'}, dimensions={0} | all-to-all | bytes 3145728 | tf_op jit(solution)/shard_map/all_to_all | solution.py:41
  41.9 0.1 reduce_sum.45
  42.0 0.0 copy-start.1
  42.2 0.5 fusion.16
  42.7 0.0 copy-done.1
  42.8 0.2 concatenate.14
  43.0 17.3 %all_to_all.26 = f32[32,33,1,128]{3,2,1,0:T(1,128)S(1)} all-to-all(f32[32,33,1,128]{3,2,1,0:T(1,128)S(1)} %bitcast.14), channel_id=1, replica_groups=mesh['zh'=4,'zl'=4,'x'=4,'y'=4,'core'=2] {'x','y','core'}, dimensions={0} | all-to-all | bytes 1081344 | tf_op jit(solution)/shard_map/all_to_all | solution.py:41
  60.3 0.3 reduce_sum.47
  60.6 24.9 %all_to_all.27 = f32[4,33,1,128]{3,2,1,0:T(1,128)S(1)} all-to-all(f32[4,33,1,128]{3,2,1,0:T(1,128)S(1)} %broadcast_in_dim.52), channel_id=1, replica_groups=mesh['zh'=4,'zl'=4,'x'=4,'y'=4,'core'=2] {'zh'}, dimensions={0} | all-to-all | bytes 135168 | tf_op jit(solution)/shard_map/all_to_all | solution.py:41
  85.5 0.1 reduce_sum.48
  85.6 7.3 %all_to_all.28 = f32[4,33,1,128]{3,2,1,0:T(1,128)S(1)} all-to-all(f32[4,33,1,128]{3,2,1,0:T(1,128)S(1)} %broadcast_in_dim.53), channel_id=1, replica_groups=mesh['zh'=4,'zl'=4,'x'=4,'y'=4,'core'=2] {'zl'}, dimensions={0} | all-to-all | bytes 135168 | tf_op jit(solution)/shard_map/all_to_all | solution.py:41
  93.0 0.1 reduce_sum.49
  93.0 0.3 broadcast_in_dim.54
  93.3 18.6 %all_to_all.29 = f32[32,33,1,128]{3,2,1,0:T(1,128)S(1)} all-to-all(f32[32,33,1,128]{3,2,1,0:T(1,128)S(1)} %broadcast_in_dim.54), channel_id=1, replica_groups=mesh['zh'=4,'zl'=4,'x'=4,'y'=4,'core'=2] {'x','y','core'}, dimensions={0} | all-to-all | bytes 1081344 | tf_op jit(solution)/shard_map/all_to_all | solution.py:41
  112.0 17.7 %factor_rows.1 = f32[32,512]{1,0:T(8,128)} custom-call(s32[1]{0:T(128)} %bitcast.1.slab_ref, f32[1056,128]{1,0:T(8,128)S(1)} %bitcast.12), custom_call_target="tpu_custom_call" | custom-call | tf_op jit(solution)/shard_map/factor_rows/pallas_call | solution.py:178
  (18 shorter events, 0.3 us)
Async XLA Ops:
  0.6 1.4 %copy-start = (bf16[1536,512]{1,0:T(8,128)(2,1)S(1)}, bf16[1536,512]{1,0:T(8,128)(2,1)}, u32[]{:S(2)}) copy-start(bf16[1536,512]{1,0:T(8,128)(2,1)} %param.3) | copy-start | bytes 4718596
  2.0 12.3 %copy-start.2 = (s32[1536]{0:T(1024)S(1)}, s32[1536]{0:T(1024)}, u32[]{:S(2)}) copy-start(s32[1536]{0:T(1024)} %param.5) | copy-start | bytes 18436
  2.0 12.3 %copy-start.3 = (bf16[1536]{0:T(1024)(128)(2,1)S(1)}, bf16[1536]{0:T(1024)(128)(2,1)}, u32[]{:S(2)}) copy-start(bf16[1536]{0:T(1024)(128)(2,1)} %param.4) | copy-start | bytes 9220
  5.4 12.0 %collective-permute-start = (f32[768,512]{1,0:T(8,128)}, f32[768,512]{1,0:T(8,128)S(1)}, u32[]{:S(2)}, u32[]{:S(2)}) collective-permute-start(f32[768,512]{1,0:T(8,128)} %fusion.1), channel_id=1, source_target_pairs={{0,1},{1,0},{2,3},{3,2},{4,5},{5,4},{6,7},{7,6},{8,9},{9,8},{10,11... | collective-permute-start | bytes 4718600 | tf_op jit(solution)/shard_map/ppermute | solution.py:196
  42.0 0.7 copy-start.1

commit v6 on v5

--- a/solution.py
+++ b/solution.py
@@ -145,13 +145,7 @@
                     work[at[b, j], later:, :] = work[at[b, j], later:, :] - update[later:, :]
         for i in range(b + 1, count):
             for j in range(i, count):
-                work[at[i, j]] = work[at[i, j]] - lax.dot_general(
-                    work[at[b, i]],
-                    work[at[b, j]],
-                    (((0,), (0,)), ((), ())),
-                    precision=lax.Precision.HIGHEST,
-                    preferred_element_type=jnp.float32,
-                )
+                work[at[i, j]] = work[at[i, j]] - rank_update(work[at[b, i]], work[at[b, j]])
     slab = slab_ref[0]
     height = out_ref.shape[0]
     per_tile = TILE // height

time: 130 us -> 130 us (level)
  no operation moved by 1% of the time
where the time goes in v6:
time: 130 us
  blocking collectives  92.2 us (71%)
  Pallas kernels  17.6 us (14%)
  starting transfers between devices  8.79 us (7%)
  matrix products  5.24 us (4%)
  local copies, waits for them, and re-layouts  2.05 us (2%)
  waiting for transfers between devices  1.62 us (1%)
    all_to_all x5, blocking collectives, exchange(): return lax.all_to_all(value, axes, split_axis=0, concat_axis=0, tiled=True)  92.2 us
    pallas_call x1, Pallas kernels, factor_rows(): pl.pallas_call(functools.partial(factor_kernel, count=cols // TILE, scale...  17.6 us
    ppermute x1, starting transfers between devices, per_device(): from_pair = lax.ppermute(theirs, 'core', [(0, 1), (1, 0)])  8.79 us
    dot_general x2, matrix products, bucket_sums(): return jnp.dot(table, design, preferred_element_type=jnp.float32)  4.78 us
  transfers between devices with their start and end apart: 1, of which 1 were waited for; matrix products, arithmetic and copies ran while one was open for 1% of the time, Pallas kernels for 0%

profile of v6, /device:TPU:1, one launch (start us, length us, event | category | flops | bytes accessed | tf_op | source)
XLA Modules:
  0.0 129.6 jit_solution(13069439978920620097)
XLA Ops:
  0.6 0.0 copy-start
  0.7 0.1 iota_add_fusion
  0.7 0.1 add.48
  0.8 1.2 copy-done
  2.0 0.0 copy-start.2
  2.0 0.0 copy-start.3
  2.0 3.4 %fusion.1 = f32[768,512]{1,0:T(8,128)} fusion(bf16[1536,512]{1,0:T(8,128)(2,1)S(1)} %copy-done, s32[1536]{0:T(1024)} %param.5, s32[768]{0:T(1024)S(1)} %add.48, bf16[1536]{0:T(1024)(128)(2,1)} %param.4), kind=kOutput, calls=%fused_computation.3 | convolution fusion | flops 1210318848 | bytes 3158016 | tf_op jit(solution)/shard_map/dot_general | solution.py:63
  5.4 8.8 %collective-permute-start = (f32[768,512]{1,0:T(8,128)}, f32[768,512]{1,0:T(8,128)S(1)}, u32[]{:S(2)}, u32[]{:S(2)}) collective-permute-start(f32[768,512]{1,0:T(8,128)} %fusion.1), channel_id=1, source_target_pairs={{0,1},{1,0},{2,3},{3,2},{4,5},{5,4},{6,7},{7,6},{8,9},{9,8},{10,11... | collective-permute-start | bytes 4718600 | tf_op jit(solution)/shard_map/ppermute | solution.py:190
  14.2 0.1 iota_add_fusion.1
  14.3 0.1 add.44
  14.4 0.0 copy-done.2
  14.4 0.0 copy-done.3
  14.4 1.4 %fusion = f32[768,512]{1,0:T(8,128)S(1)} fusion(bf16[1536,512]{1,0:T(8,128)(2,1)S(1)} %copy-done, s32[1536]{0:T(1024)S(1)} %copy-done.2, s32[768]{0:T(1024)S(1)} %add.44, bf16[1536]{0:T(1024)(128)(2,1)S(1)} %copy-done.3), kind=kOutput, calls=%fused_computation.2 | convolution fusion | flops 1210318848 | bytes 3158016 | tf_op jit(solution)/shard_map/dot_general | solution.py:63
  15.8 1.6 %collective-permute-done = f32[768,512]{1,0:T(8,128)S(1)} collective-permute-done((f32[768,512]{1,0:T(8,128)}, f32[768,512]{1,0:T(8,128)S(1)}, u32[]{:S(2)}, u32[]{:S(2)}) %collective-permute-start) | collective-permute-done | bytes 1572896 | tf_op jit(solution)/shard_map/ppermute | solution.py:190
  17.4 0.3 add.49
  17.8 24.1 %all_to_all.25 = f32[16,48,512]{2,1,0:T(8,128)S(1)} all-to-all(f32[16,48,512]{2,1,0:T(8,128)S(1)} %bitcast.13), channel_id=1, replica_groups=mesh['zh'=4,'zl'=4,'x'=4,'y'=4,'core'=2] {'x','y'}, dimensions={0} | all-to-all | bytes 3145728 | tf_op jit(solution)/shard_map/all_to_all | solution.py:41
  41.9 0.1 reduce_sum.45
  42.0 0.0 copy-start.1
  42.2 0.5 fusion.16
  42.7 0.0 copy-done.1
  42.8 0.2 concatenate.14
  43.0 17.3 %all_to_all.26 = f32[32,33,1,128]{3,2,1,0:T(1,128)S(1)} all-to-all(f32[32,33,1,128]{3,2,1,0:T(1,128)S(1)} %bitcast.14), channel_id=1, replica_groups=mesh['zh'=4,'zl'=4,'x'=4,'y'=4,'core'=2] {'x','y','core'}, dimensions={0} | all-to-all | bytes 1081344 | tf_op jit(solution)/shard_map/all_to_all | solution.py:41
  60.3 0.3 reduce_sum.47
  60.6 24.9 %all_to_all.27 = f32[4,33,1,128]{3,2,1,0:T(1,128)S(1)} all-to-all(f32[4,33,1,128]{3,2,1,0:T(1,128)S(1)} %broadcast_in_dim.52), channel_id=1, replica_groups=mesh['zh'=4,'zl'=4,'x'=4,'y'=4,'core'=2] {'zh'}, dimensions={0} | all-to-all | bytes 135168 | tf_op jit(solution)/shard_map/all_to_all | solution.py:41
  85.5 0.1 reduce_sum.48
  85.6 7.3 %all_to_all.28 = f32[4,33,1,128]{3,2,1,0:T(1,128)S(1)} all-to-all(f32[4,33,1,128]{3,2,1,0:T(1,128)S(1)} %broadcast_in_dim.53), channel_id=1, replica_groups=mesh['zh'=4,'zl'=4,'x'=4,'y'=4,'core'=2] {'zl'}, dimensions={0} | all-to-all | bytes 135168 | tf_op jit(solution)/shard_map/all_to_all | solution.py:41
  93.0 0.1 reduce_sum.49
  93.0 0.3 broadcast_in_dim.54
  93.3 18.6 %all_to_all.29 = f32[32,33,1,128]{3,2,1,0:T(1,128)S(1)} all-to-all(f32[32,33,1,128]{3,2,1,0:T(1,128)S(1)} %broadcast_in_dim.54), channel_id=1, replica_groups=mesh['zh'=4,'zl'=4,'x'=4,'y'=4,'core'=2] {'x','y','core'}, dimensions={0} | all-to-all | bytes 1081344 | tf_op jit(solution)/shard_map/all_to_all | solution.py:41
  112.0 17.6 %factor_rows.1 = f32[32,512]{1,0:T(8,128)} custom-call(s32[1]{0:T(128)} %bitcast.1.slab_ref, f32[1056,128]{1,0:T(8,128)S(1)} %bitcast.12), custom_call_target="tpu_custom_call" | custom-call | tf_op jit(solution)/shard_map/factor_rows/pallas_call | solution.py:172
  (18 shorter events, 0.3 us)
Async XLA Ops:
  0.6 1.4 %copy-start = (bf16[1536,512]{1,0:T(8,128)(2,1)S(1)}, bf16[1536,512]{1,0:T(8,128)(2,1)}, u32[]{:S(2)}) copy-start(bf16[1536,512]{1,0:T(8,128)(2,1)} %param.3) | copy-start | bytes 4718596
  2.0 12.3 %copy-start.2 = (s32[1536]{0:T(1024)S(1)}, s32[1536]{0:T(1024)}, u32[]{:S(2)}) copy-start(s32[1536]{0:T(1024)} %param.5) | copy-start | bytes 18436
  2.0 12.3 %copy-start.3 = (bf16[1536]{0:T(1024)(128)(2,1)S(1)}, bf16[1536]{0:T(1024)(128)(2,1)}, u32[]{:S(2)}) copy-start(bf16[1536]{0:T(1024)(128)(2,1)} %param.4) | copy-start | bytes 9220
  5.4 12.0 %collective-permute-start = (f32[768,512]{1,0:T(8,128)}, f32[768,512]{1,0:T(8,128)S(1)}, u32[]{:S(2)}, u32[]{:S(2)}) collective-permute-start(f32[768,512]{1,0:T(8,128)} %fusion.1), channel_id=1, source_target_pairs={{0,1},{1,0},{2,3},{3,2},{4,5},{5,4},{6,7},{7,6},{8,9},{9,8},{10,11... | collective-permute-start | bytes 4718600 | tf_op jit(solution)/shard_map/ppermute | solution.py:190
  42.0 0.7 copy-start.1
